TPU v7x, 512 devices: a whole 4x4x16 slice. The times are simulated.
512 devices in a mesh: group: 8 (over x, core), dom: 64 (over y, z).
Axes of the slice: x: 4, y: 4, z: 16, core: 2. Of those that a mesh axis runs over, the one named last changes fastest.
Arguments:
- density_modes: float32 [64, 65536], P(None, ('group', 'dom')), may hold values from -4 to 4, as said below
- wave_speed: float32 [65536], P(('group', 'dom')), may hold values from 0.5 to 8
- shock_flags: int32 [65536], P(('group', 'dom')), may hold values 0 or 1
- elem_mass: float32 [65536], P(('group', 'dom')), may hold values from 0.2 to 1
- stiff_eigs: float32 [64], replicated, may hold values from 0.1 to 20
- coupling: bfloat16 [64, 96, 65536], P(None, None, ('group', 'dom')), may hold values from -3 to 3
- interior_res: float32 [5, 64, 65536], P(None, None, ('group', 'dom')), may hold values from -6 to 6
- face_res: float32 [5, 96, 65536], P(None, None, ('group', 'dom')), may hold values from -6 to 6
- send_rows: int32 [786432], P(('group', 'dom')), may hold values from 0 to 768, as said below
- face_rows: int32 [2, 393216], P(None, ('group', 'dom')), may hold values from 0 to 1536, as said below
Outputs:
- elem_update: float32 [5, 64, 65536], P(None, None, ('group', 'dom'))
- slot_traces: float32 [5, 96, 65536], P(None, None, ('group', 'dom'))
Inputs may be any that keep to these rules, and one draw needn't show every extreme that they name: `density_modes`: mode coefficients of each element fall with polynomial degree at an element's own rate. `send_rows`: A device's block lists, at position q * 24 + i, the slot it sends as the i-th to the device of dom index q in its own group, or 768 for an empty position. Every slot appears exactly once. At most 24 slots go from one device to one owner, and in every group two owners receive 24 from every device of the group. `face_rows`: each received row that carries a slot is named exactly once in its device's block; unused faces hold 1536 in both entries; in every group some device uses all 768 faces.
All inputs are finite; a program needn't handle non-finite values. No bound on the sum of `shock_flags` on one device may be relied on, other than what follows from the above.
Results may differ from a plain program's by a relative error of at most 0.0003.
Values sent between devices are 32-bit elements; how exact they have to be, the bound alone decides.
A program may use at most 64 MiB of HBM per device.

v0:
```python
import jax
import jax.numpy as jnp
from jax import lax
from jax.sharding import PartitionSpec as P

MODES = 64
FNODES = 16
COMPS = 5
EFACES = 6


EPS_SCALE = 0.1
NU_BASE = 0.02
TAU_STAB = 1.0
SENSOR_MID = -2.0
SENSOR_WIDTH = 0.5
RATIO_FLOOR = 0.0001


def sensor_visc(density_modes, wave_speed, shock_flags):
    mode_ids = jnp.arange(MODES, dtype=jnp.int32)
    degree = jnp.maximum(jnp.maximum(mode_ids // 16, mode_ids // 4 % 4), mode_ids % 4)
    top_mask = (degree == 3).astype(jnp.float32)
    squares = density_modes * density_modes
    totals = jnp.sum(squares, axis=0) + 1e-06
    high_part = jnp.sum(squares * top_mask[:, None], axis=0)
    sensor = jnp.log10(jnp.maximum(high_part / totals, RATIO_FLOOR))
    ramped = 0.5 * (1.0 + jnp.tanh((sensor - SENSOR_MID) / SENSOR_WIDTH))
    return EPS_SCALE * wave_speed * jnp.maximum(ramped, 0.5 * shock_flags.astype(jnp.float32))


def element_terms(coupling, c_coef, interior_res, face_res):
    widened = coupling.astype(jnp.float32)
    scaled = widened * c_coef[:, None, :]
    width_n = widened.shape[2]
    shaped_full = widened.reshape(MODES, EFACES, FNODES, width_n)
    shaped_scaled = scaled.reshape(MODES, EFACES, FNODES, width_n)
    blocks = jnp.einsum(
        "kjan,kjbn->jabn", shaped_scaled, shaped_full, precision=lax.Precision.HIGHEST
    )
    blocks = blocks + TAU_STAB * jnp.eye(FNODES, dtype=jnp.float32)[None, :, :, None]
    weighted = c_coef[None, :, :] * interior_res
    loads = face_res - jnp.einsum(
        "ktn,ckn->ctn", widened, weighted, precision=lax.Precision.HIGHEST
    )
    return (blocks, loads)


def back_substitute(coupling, c_coef, interior_res, traces):
    widened = coupling.astype(jnp.float32)
    pulled = jnp.einsum("kte,cte->cke", widened, traces, precision=lax.Precision.HIGHEST)
    return c_coef[None, :, :] * (interior_res - pulled)


def cholesky_solve(matrix, eye_fill, rhs_part):
    order_n = matrix.shape[0]
    factor = [[None] * order_n for _ in range(order_n)]
    for i in range(order_n):
        for j in range(i + 1):
            accum = matrix[i, j]
            if i == j:
                accum = accum + eye_fill
            for k in range(j):
                accum = accum - factor[i][k] * factor[j][k]
            if i == j:
                factor[i][i] = jnp.sqrt(accum)
            else:
                factor[i][j] = accum / factor[j][j]
    forward = []
    for i in range(order_n):
        accum = rhs_part[:, i]
        for k in range(i):
            accum = accum - factor[i][k][None, :] * forward[k]
        forward.append(accum / factor[i][i][None, :])
    backward = [None] * order_n
    for i in reversed(range(order_n)):
        accum = forward[i]
        for k in range(i + 1, order_n):
            accum = accum - factor[k][i][None, :] * backward[k]
        backward[i] = accum / factor[i][i][None, :]
    return jnp.stack(backward, axis=1)


def solve_packed(packed, usable, block_width):
    full_block = packed[:, : FNODES * FNODES]
    matrix = jnp.transpose(full_block).reshape(FNODES, FNODES, -1)
    eye_fill = 1.0 - usable.astype(jnp.float32)
    rhs_part = jnp.transpose(packed[:, block_width : block_width + COMPS * FNODES]).reshape(
        COMPS, FNODES, -1
    )
    solved = cholesky_solve(matrix, eye_fill, rhs_part)
    return jnp.transpose(solved.reshape(COMPS * FNODES, -1))


def local(
    density_modes,
    wave_speed,
    shock_flags,
    elem_mass,
    stiff_eigs,
    coupling,
    interior_res,
    face_res,
    send_rows,
    face_rows,
):
    elements = wave_speed.shape[0]
    slot_total = EFACES * elements
    dom_size = lax.axis_size("dom")
    row_total = send_rows.shape[0]
    capacity = row_total // dom_size
    face_total = face_rows.shape[1]
    peak = lax.pmax(jnp.max(wave_speed), ("group", "dom"))
    viscous = sensor_visc(density_modes, wave_speed, shock_flags)
    row_ids = jnp.arange(row_total, dtype=jnp.int32)
    sent_ok = send_rows < slot_total
    sent_slot = jnp.minimum(send_rows, slot_total - 1)
    slot_place = jnp.zeros((slot_total,), jnp.int32).at[send_rows].set(row_ids, mode="drop")
    first_row = face_rows[0]
    second_row = face_rows[1]
    face_ok = first_row < row_total
    first_clip = jnp.minimum(first_row, row_total - 1)
    second_clip = jnp.minimum(second_row, row_total - 1)
    face_ids = jnp.arange(face_total, dtype=jnp.int32)
    row_face = (
        jnp.full((row_total,), face_total, jnp.int32)
        .at[first_row]
        .set(face_ids, mode="drop")
        .at[second_row]
        .set(face_ids, mode="drop")
    )
    row_ok = row_face < face_total
    row_clip = jnp.minimum(row_face, face_total - 1)
    eps_slots = jnp.tile(viscous, EFACES)
    outgoing = jnp.where(sent_ok, eps_slots[sent_slot], 0.0).reshape(dom_size, capacity)
    arrived = lax.all_to_all(outgoing, "dom", split_axis=0, concat_axis=0, tiled=True).reshape(
        row_total
    )
    face_visc = 0.5 * (arrived[first_clip] + arrived[second_clip])
    returning = jnp.where(row_ok, face_visc[row_clip], 0.0).reshape(dom_size, capacity)
    came_back = lax.all_to_all(returning, "dom", split_axis=0, concat_axis=0, tiled=True).reshape(
        row_total
    )
    slot_visc = came_back[slot_place]
    nu_elem = NU_BASE + jnp.mean(slot_visc.reshape(EFACES, elements), axis=0)
    c_coef = 1.0 / (
        elem_mass[None, :]
        * (1.0 + wave_speed[None, :] / peak + nu_elem[None, :] * stiff_eigs[:, None])
    )
    blocks, loads = element_terms(coupling, c_coef, interior_res, face_res)
    flat_blocks = blocks.reshape(EFACES, FNODES * FNODES, elements)
    block_width = flat_blocks.shape[1]
    load_part = (
        loads.reshape(COMPS, EFACES, FNODES, elements)
        .transpose(1, 0, 2, 3)
        .reshape(EFACES, COMPS * FNODES, elements)
    )
    used_width = block_width + COMPS * FNODES
    width_total = (used_width + 127) // 128 * 128
    padding = jnp.zeros((EFACES, width_total - used_width, elements), jnp.float32)
    payload = (
        jnp.concatenate([flat_blocks, load_part, padding], axis=1)
        .transpose(0, 2, 1)
        .reshape(slot_total, width_total)
    )
    outgoing_blocks = jnp.where(sent_ok[:, None], payload[sent_slot], 0.0).reshape(
        dom_size, capacity, width_total
    )
    arrived_blocks = lax.all_to_all(
        outgoing_blocks, "dom", split_axis=0, concat_axis=0, tiled=True
    ).reshape(row_total, width_total)
    summed = jnp.where(
        face_ok[:, None], arrived_blocks[first_clip] + arrived_blocks[second_clip], 0.0
    )
    face_trace = solve_packed(summed, face_ok, block_width)
    trace_width = (COMPS * FNODES + 127) // 128 * 128
    padded_trace = jnp.concatenate(
        [face_trace, jnp.zeros((face_total, trace_width - COMPS * FNODES), jnp.float32)], axis=1
    )
    returning_traces = jnp.where(row_ok[:, None], padded_trace[row_clip], 0.0).reshape(
        dom_size, capacity, trace_width
    )
    back_traces = lax.all_to_all(
        returning_traces, "dom", split_axis=0, concat_axis=0, tiled=True
    ).reshape(row_total, trace_width)
    slot_trace = back_traces[slot_place][:, : COMPS * FNODES]
    traces = (
        slot_trace.reshape(EFACES, elements, COMPS, FNODES)
        .transpose(2, 0, 3, 1)
        .reshape(COMPS, EFACES * FNODES, elements)
    )
    update = back_substitute(coupling, c_coef, interior_res, traces)
    return (update, traces)


def solution(mesh):
    return jax.shard_map(
        local,
        mesh=mesh,
        in_specs=(
            P(None, ("group", "dom")),
            P(("group", "dom")),
            P(("group", "dom")),
            P(("group", "dom")),
            P(),
            P(None, None, ("group", "dom")),
            P(None, None, ("group", "dom")),
            P(None, None, ("group", "dom")),
            P(("group", "dom")),
            P(None, ("group", "dom")),
        ),
        out_specs=(P(None, None, ("group", "dom")), P(None, None, ("group", "dom"))),
        check_vma=False,
    )
```

profile of v0, /device:TPU:24, one launch (start us, length us, event | category | flops | bytes accessed | tf_op | source)
XLA Modules:
  0.0 428.1 jit_solution(15227957402505525768)
XLA Ops:
  0.6 1.3 reduce_max.9
  1.9 108.0 %pmax.7 = f32[]{:T(128)} all-reduce(f32[]{:T(128)} %reduce_max.9), channel_id=1, replica_groups=mesh['group'=8,'dom'=64] {'group','dom'}, use_global_device_ids=true, to_apply=%region_1.0 | all-reduce | flops 1 | bytes 8 | tf_op jit(solution)/shard_map/pmax | solution.py:113
  109.9 0.9 multiply_reduce_fusion.1
  110.7 1.3 divide_add_fusion
  112.1 0.7 compare_select_fusion
  112.8 5.9 %gather_fusion = f32[1536]{0:T(1024)S(1)} fusion(f32[768]{0:T(1024)S(1)} %broadcast_bitcast_fusion, s32[2048]{0:T(1024)S(1)} %pad_clamp_fusion.1), kind=kCustom, calls=%fused_computation | custom fusion | bytes 18432 | tf_op jit(solution)/shard_map/gather | solution.py:135
  118.7 0.7 all_to_all.18
  119.4 11.4 %all-to-all-start = ((f32[64,1,24]{2,1,0:T(1,128)}), f32[64,1,24]{2,1,0:T(1,128)S(1)}, u32[]{:S(2)}, u32[]{:S(2)}) async-start(f32[64,1,24]{2,1,0:T(1,128)} %bitcast.3), calls=%async_computation | async-start | bytes 65536 | tf_op jit(solution)/shard_map/all_to_all | solution.py:136
  130.9 3.4 scatter_custom_fusion
  134.3 3.4 scatter_fusion
  137.8 6.2 %scatter_custom_fusion.2 = s32[768]{0:T(1024)S(1)} fusion(s32[1536]{0:T(1024)S(1)} %get-tuple-element.456, s32[1536]{0:T(1024)S(1)} %iota.30, s32[]{:T(128)} %constant.71.clone.1), kind=kCustom, calls=%fused_computation.1000 | custom fusion | bytes 3076 | tf_op jit(solution)/shard_map/scatter | solution.py:118
  144.0 0.6 broadcast.9756
  144.6 0.7 reduce.286
  145.4 4.5 %gather_fusion.1 = f32[768]{0:T(1024)S(1)} fusion(f32[1536]{0:T(1024)S(1)} %reshape.18244, s32[1024]{0:T(1024)S(1)} %pad_clamp_fusion.4), kind=kCustom, calls=%fused_computation.1 | custom fusion | bytes 9216 | tf_op jit(solution)/shard_map/gather | solution.py:139
  149.9 4.5 %gather_fusion.2 = f32[768]{0:T(1024)S(1)} fusion(f32[1536]{0:T(1024)S(1)} %reshape.18244, s32[1024]{0:T(1024)S(1)} %pad_clamp_fusion.3), kind=kCustom, calls=%fused_computation.2 | custom fusion | bytes 9216 | tf_op jit(solution)/shard_map/gather | solution.py:139
  154.4 5.9 %gather_fusion.3 = f32[1536]{0:T(1024)S(1)} fusion(f32[768]{0:T(1024)S(1)} %add_multiply_fusion, s32[2048]{0:T(1024)S(1)} %pad_clamp_fusion), kind=kCustom, calls=%fused_computation.3 | custom fusion | bytes 18432 | tf_op jit(solution)/shard_map/gather | solution.py:140
  160.2 0.6 broadcast_select_fusion.1
  160.8 0.7 all_to_all.20
  161.5 15.1 %all-to-all-start.1 = ((f32[64,1,24]{2,1,0:T(1,128)}), f32[64,1,24]{2,1,0:T(1,128)S(1)}, u32[]{:S(2)}, u32[]{:S(2)}) async-start(f32[64,1,24]{2,1,0:T(1,128)} %bitcast.4), calls=%async_computation.1 | async-start | bytes 65536 | tf_op jit(solution)/shard_map/all_to_all | solution.py:141
  176.7 3.2 copy.329
  179.9 0.2 copy.398
  180.2 6.5 %copy.326 = bf16[64,6,16,128]{0,2,3,1:T(8,128)(2,1)} copy(bf16[64,6,16,128]{3,2,1,0:T(8,128)(2,1)} %bitcast.2106) | data formatting | bytes 3145728 | tf_op jit(solution)/shard_map/reshape | solution.py:36
  186.8 0.7 broadcast_in_dim.56
  187.4 1.7 all-to-all-done.1
  189.2 0.7 reduce.287
  190.0 4.5 %gather_fusion.4 = f32[768]{0:T(1024)S(1)} fusion(f32[1536]{0:T(1024)S(1)} %reshape.18245, s32[1024]{0:T(1024)S(1)} %pad_clamp_fusion.2), kind=kCustom, calls=%fused_computation.4 | custom fusion | bytes 9216 | tf_op jit(solution)/shard_map/gather | solution.py:144
  194.7 3.6 convert_multiply_fusion
  198.3 1.8 fusion.2
  200.3 6.9 %copy.325 = f32[64,6,16,128]{0,2,3,1:T(8,128)} copy(f32[64,6,16,128]{3,2,1,0:T(8,128)} %bitcast.2107) | data formatting | bytes 6291456 | tf_op jit(solution)/shard_map/reshape | solution.py:37
  207.3 8.7 %add_bitcast_fusion = f32[6,16,16,128]{2,1,3,0:T(8,128)} fusion(f32[16,16]{1,0:T(8,128)S(1)} %fusion.173, f32[64,6,16,128]{0,2,3,1:T(8,128)} %copy.325, bf16[64,6,16,128]{0,2,3,1:T(8,128)(2,1)S(1)} %copy-done.2), kind=kOutput, calls=%fused_computation.13 | convolution fusion | flops 151191552 | bytes 5506048 | tf_op jit(solution)/shard_map/kjan,kjbn->jabn/dot_general | solution.py:38
  215.9 4.6 %copy.327 = f32[6,16,16,128]{3,2,1,0:T(8,128)S(1)} copy(f32[6,16,16,128]{2,1,3,0:T(8,128)} %add_bitcast_fusion) | data formatting | bytes 1572864 | tf_op jit(solution)/shard_map/add | solution.py:41
  220.7 0.4 copy.332
  221.0 3.7 gather_fusion.5
  224.8 2.4 broadcast_select_fusion
  227.2 13.5 %all-to-all-start.2 = ((f32[64,24,384]{2,1,0:T(8,128)}), f32[64,24,384]{2,1,0:T(8,128)S(1)}, u32[]{:S(2)}, u32[]{:S(2)}) async-start(f32[64,24,384]{2,1,0:T(8,128)} %broadcast_select_fusion), calls=%async_computation.2 | async-start | bytes 4718592 | tf_op jit(solution)/shard_map/all_to_all | solution.py:169
  240.7 0.6 compare_reduce_fusion
  241.3 107.6 %all-to-all-done.2 = f32[64,24,384]{2,1,0:T(8,128)S(1)} async-done(((f32[64,24,384]{2,1,0:T(8,128)}), f32[64,24,384]{2,1,0:T(8,128)S(1)}, u32[]{:S(2)}, u32[]{:S(2)}) %all-to-all-start.2) | async-done | bytes 2359328 | tf_op jit(solution)/shard_map/all_to_all | solution.py:169
  348.9 2.1 gather_fusion.7
  351.0 3.0 gather_fusion.6
  354.0 1.4 add_select_fusion
  355.6 0.3 copy.335
  356.4 0.3 multiply_reduce_fusion.117
  356.8 0.3 multiply_reduce_fusion.116
  357.1 0.4 multiply_reduce_fusion.115
  357.5 0.4 multiply_reduce_fusion.114
  357.9 0.4 multiply_reduce_fusion.113
  358.3 0.4 multiply_reduce_fusion.112
  358.7 0.3 multiply_reduce_fusion.111
  359.1 0.3 multiply_reduce_fusion.110
  359.5 0.3 multiply_reduce_fusion.109
  359.9 0.4 multiply_reduce_fusion.2
  361.0 1.5 subtract_divide_fusion
  362.5 0.8 divide_bitcast_fusion
  363.4 1.0 subtract_divide_fusion.27
  364.4 1.3 subtract_divide_fusion.14
  365.7 0.4 stack.11
  366.3 2.6 gather_fusion.8
  368.9 0.3 pad_select_fusion
  369.2 50.2 %all_to_all.28 = f32[64,24,128]{2,1,0:T(8,128)S(1)} all-to-all(f32[64,24,128]{2,1,0:T(8,128)S(1)} %bitcast.2110), channel_id=1, replica_groups=mesh['group'=8,'dom'=64] {'dom'}, dimensions={0} | all-to-all | bytes 1572864 | tf_op jit(solution)/shard_map/all_to_all | solution.py:183
  419.4 1.6 gather_fusion.9
  421.3 1.0 copy.396
  422.3 0.6 copy-done.1
  422.9 4.4 %fusion.1 = f32[5,64,128]{1,0,2:T(8,128)S(1)} fusion(f32[5,64,128]{1,0,2:T(8,128)S(1)} %copy-done.4, f32[5,96,128]{1,0,2:T(8,128)} %copy.396, bf16[64,96,128]{1,0,2:T(8,128)(2,1)S(1)} %copy-done.1, f32[64,128]{0,1:T(8,128)S(1)} %copy-done.7), kind=kOutput, calls=%fused_computation.17 | convolution fusion | flops 47267840 | bytes 2179072 | tf_op jit(solution)/shard_map/kte,cte->cke/dot_general | solution.py:51
  427.3 0.9 copy.399
  (112 shorter events, 3.0 us)
Async XLA Ops:
  112.8 5.9 %copy-start.19 = (s32[1536]{0:T(1024)S(1)}, s32[1536]{0:T(1024)}, u32[]{:S(2)}) copy-start(s32[1536]{0:T(1024)} %param.18) | copy-start | bytes 18436
  112.8 18.0 %copy-start.8 = (s32[2,768]{1,0:T(2,128)S(1)}, s32[2,768]{1,0:T(2,128)}, u32[]{:S(2)}) copy-start(s32[2,768]{1,0:T(2,128)} %param.19) | copy-start | bytes 18436
  119.4 24.6 %all-to-all-start = ((f32[64,1,24]{2,1,0:T(1,128)}), f32[64,1,24]{2,1,0:T(1,128)S(1)}, u32[]{:S(2)}, u32[]{:S(2)}) async-start(f32[64,1,24]{2,1,0:T(1,128)} %bitcast.3), calls=%async_computation | async-start | bytes 65536 | tf_op jit(solution)/shard_map/all_to_all | solution.py:136
  130.9 14.5 %copy-start.13 = (s32[1024]{0:T(1024)}, s32[1024]{0:T(1024)S(1)}, u32[]{:S(2)}) copy-start(s32[1024]{0:T(1024)S(1)} %pad_clamp_fusion.4) | copy-start | bytes 12292
  137.8 16.6 %copy-start.11 = (s32[2048]{0:T(1024)}, s32[2048]{0:T(1024)S(1)}, u32[]{:S(2)}) copy-start(s32[2048]{0:T(1024)S(1)} %pad_clamp_fusion) | copy-start | bytes 24580
  144.0 5.9 %copy-start.15 = (s32[1024]{0:T(1024)}, s32[1024]{0:T(1024)S(1)}, u32[]{:S(2)}) copy-start(s32[1024]{0:T(1024)S(1)} %pad_clamp_fusion.3) | copy-start | bytes 12292
  160.2 19.7 %copy-start.10 = (f32[5,64,128]{2,1,0:T(8,128)S(1)}, f32[5,64,128]{2,1,0:T(8,128)}, u32[]{:S(2)}) copy-start(f32[5,64,128]{2,1,0:T(8,128)} %param.16) | copy-start | bytes 491524
  161.5 27.6 %all-to-all-start.1 = ((f32[64,1,24]{2,1,0:T(1,128)}), f32[64,1,24]{2,1,0:T(1,128)S(1)}, u32[]{:S(2)}, u32[]{:S(2)}) async-start(f32[64,1,24]{2,1,0:T(1,128)} %bitcast.4), calls=%async_computation.1 | async-start | bytes 65536 | tf_op jit(solution)/shard_map/all_to_all | solution.py:141
  176.7 13.3 %copy-start.17 = (s32[1024]{0:T(1024)}, s32[1024]{0:T(1024)S(1)}, u32[]{:S(2)}) copy-start(s32[1024]{0:T(1024)S(1)} %pad_clamp_fusion.2) | copy-start | bytes 12292
  179.9 18.4 %copy-start = (bf16[64,96,128]{1,0,2:T(8,128)(2,1)}, bf16[64,96,128]{1,0,2:T(8,128)(2,1)S(1)}, u32[]{:S(2)}) copy-start(bf16[64,96,128]{1,0,2:T(8,128)(2,1)S(1)} %copy.329) | copy-start | bytes 4718596
  180.2 18.1 %copy-start.3 = (f32[5,64,128]{1,0,2:T(8,128)}, f32[5,64,128]{1,0,2:T(8,128)S(1)}, u32[]{:S(2)}) copy-start(f32[5,64,128]{1,0,2:T(8,128)S(1)} %copy.398) | copy-start | bytes 491524
  190.0 4.5 %copy-start.22 = (f32[64]{0:T(128)S(1)}, f32[64]{0:T(128)}, u32[]{:S(2)}) copy-start(f32[64]{0:T(128)} %param.14) | copy-start | bytes 772
  190.0 4.5 %copy-start.23 = (f32[128]{0:T(128)S(1)}, f32[128]{0:T(128)}, u32[]{:S(2)}) copy-start(f32[128]{0:T(128)} %param.13) | copy-start | bytes 1540
  194.7 3.6 copy-start.6
  198.3 2.0 copy-start.9
  200.3 6.9 %copy-start.2 = (bf16[64,6,16,128]{0,2,3,1:T(8,128)(2,1)S(1)}, bf16[64,6,16,128]{0,2,3,1:T(8,128)(2,1)}, u32[]{:S(2)}) copy-start(bf16[64,6,16,128]{0,2,3,1:T(8,128)(2,1)} %copy.326) | copy-start | bytes 4718596
  227.2 121.7 %copy-start.16 = (s32[1024]{0:T(1024)S(1)}, s32[1024]{0:T(1024)}, u32[]{:S(2)}) copy-start(s32[1024]{0:T(1024)} %copy-done.15) | copy-start | bytes 12292
  227.2 121.7 %all-to-all-start.2 = ((f32[64,24,384]{2,1,0:T(8,128)}), f32[64,24,384]{2,1,0:T(8,128)S(1)}, u32[]{:S(2)}, u32[]{:S(2)}) async-start(f32[64,24,384]{2,1,0:T(8,128)} %broadcast_select_fusion), calls=%async_computation.2 | async-start | bytes 4718592 | tf_op jit(solution)/shard_map/all_to_all | solution.py:169
  348.9 2.1 copy-start.14
  351.0 3.0 copy-start.21
  362.5 3.8 copy-start.12
  366.3 2.6 copy-start.20
  368.9 50.5 %copy-start.18 = (s32[1024]{0:T(1024)S(1)}, s32[1024]{0:T(1024)}, u32[]{:S(2)}) copy-start(s32[1024]{0:T(1024)} %copy-done.17) | copy-start | bytes 12292
  419.4 2.9 copy-start.4
  421.0 1.9 copy-start.1
  421.0 1.9 copy-start.7
  421.3 6.0 %copy-start.5 = (f32[5,6,16,128]{3,2,1,0:T(8,128)}, f32[5,6,16,128]{3,2,1,0:T(8,128)S(1)}, u32[]{:S(2)}) copy-start(f32[5,6,16,128]{3,2,1,0:T(8,128)S(1)} %copy.395) | copy-start | bytes 737284
where the time goes:
time: 429 us; the launch traced here: 428 us
  blocking collectives  158 us (37%)
  waiting for transfers between devices  109 us (25%)
  local copies, waits for them, and re-layouts  79.9 us (19%)
  starting transfers between devices  40.1 us (9%)
  other arithmetic  24.2 us (6%)
  matrix products  14.8 us (3%)
    pmax x1, blocking collectives, local(): peak = lax.pmax(jnp.max(wave_speed), ('group', 'dom'))  108 us
    all_to_all x1, waiting for transfers between devices, local(): lax.all_to_all(outgoing_blocks, 'dom', split_axis=0, concat_axis=0, tiled...  108 us
    all_to_all x1, blocking collectives, local(): lax.all_to_all(returning_traces, 'dom', split_axis=0, concat_axis=0, tile...  50.2 us
    all_to_all x1, starting transfers between devices, local(): lax.all_to_all(returning, 'dom', split_axis=0, concat_axis=0, tiled=True)  15.1 us
    all_to_all x1, starting transfers between devices, local(): lax.all_to_all(outgoing_blocks, 'dom', split_axis=0, concat_axis=0, tiled...  13.5 us
    all_to_all x1, starting transfers between devices, local(): lax.all_to_all(outgoing, 'dom', split_axis=0, concat_axis=0, tiled=True)  11.4 us
    gather x2, local copies, waits for them, and re-layouts, local(): face_visc = 0.5 * (arrived[first_clip] + arrived[second_clip])  8.93 us
    dot_general x1, matrix products, element_terms(): jnp.einsum('kjan,kjbn->jabn', shaped_scaled, shaped_full, precision=lax.P...  8.66 us
  transfers between devices with their start and end apart: 3, of which 2 were waited for; matrix products, arithmetic and copies ran while one was open for 6% of the time, Pallas kernels for 0%

commit v1 on v0

v1 whole, which is shorter than its diff:
```python
import functools

import jax
import jax.numpy as jnp
from jax import lax
from jax.experimental import pallas as pl
from jax.experimental.pallas import tpu as pltpu
from jax.sharding import PartitionSpec as P

MODES = 64
FNODES = 16
COMPS = 5
EFACES = 6
TRACE = 96
ELEM_DEV = 128
SLOTS = EFACES * ELEM_DEV
CAP = 24
N_DOM = 64
N_GROUP = 8
ROWS = N_DOM * CAP
FACES = 768
TRI = 136
WIDE = 256
LANES = 128
OUT_TILE = 40
RET_TILE = 16

EPS_SCALE = 0.1
NU_BASE = 0.02
TAU_STAB = 1.0
SENSOR_MID = -2.0
SENSOR_WIDTH = 0.5
RATIO_FLOOR = 0.0001

F32 = jnp.float32
BF16 = jnp.bfloat16
I32 = jnp.int32
MESH = pl.DeviceIdType.MESH
NN = (((1,), (0,)), ((), ()))
NT = (((1,), (1,)), ((), ()))
VMEM_LIMIT = 60 * 1024 * 1024


def iota(shape, axis):
    return lax.broadcasted_iota(I32, shape, axis)


def split3(x):
    high = x.astype(BF16)
    rest = x - high.astype(F32)
    middle = rest.astype(BF16)
    low = (rest - middle.astype(F32)).astype(BF16)
    return high, middle, low


def split2(x):
    high = x.astype(BF16)
    return high, (x - high.astype(F32)).astype(BF16)


def dot(a, b, dims):
    return lax.dot_general(a, b, dims, preferred_element_type=F32)


def one_hot(mask):
    return jnp.where(mask, 1.0, 0.0).astype(BF16)


def element_eps(density, speed, flags):
    ids = iota((MODES, LANES), 0)
    degree = jnp.maximum(jnp.maximum(ids >> 4, (ids >> 2) & 3), ids & 3)
    squares = density * density
    totals = jnp.sum(squares, axis=0, keepdims=True) + 1e-06
    high = jnp.sum(jnp.where(degree == 3, squares, 0.0), axis=0, keepdims=True)
    sensor = jnp.log10(jnp.maximum(high / totals, RATIO_FLOOR))
    ramped = 0.5 * (1.0 + jnp.tanh((sensor - SENSOR_MID) / SENSOR_WIDTH))
    return EPS_SCALE * speed * jnp.maximum(ramped, 0.5 * flags.astype(F32))


def padded_row(row):
    source = (row * 2731) >> 16
    return source, row - source * CAP


def partner_rows(face_ref, fcol_ref):
    high_parts = []
    low_parts = []
    for end in range(2):
        own_p, own_i = padded_row(face_ref[end : end + 1, :])
        other_p, other_i = padded_row(face_ref[1 - end : 2 - end, :])
        mine = iota((16, FACES), 0) == (own_p >> 2)
        high_parts.append(
            jnp.concatenate(
                [
                    jnp.where(mine, other_p.astype(F32), 0.0),
                    jnp.where(mine, other_i.astype(F32), 0.0),
                ],
                axis=0,
            ).astype(BF16)
        )
        columns = []
        for chunk in range(6):
            col_p, col_i = padded_row(fcol_ref[:, end * 6 + chunk : end * 6 + chunk + 1])
            place = ((col_p & 3) << 5) + col_i
            columns.append(one_hot(iota((LANES, LANES), 1) == place))
        low_parts.append(jnp.concatenate(columns, axis=0))
    found = dot(high_parts[0], low_parts[0], NN) + dot(high_parts[1], low_parts[1], NN)
    found = found.astype(I32)
    return found[0:16], found[16:32]


def remote(src, dst, send_sem, recv_sem, where):
    return pltpu.make_async_remote_copy(
        src_ref=src,
        dst_ref=dst,
        send_sem=send_sem,
        recv_sem=recv_sem,
        device_id=where,
        device_id_type=MESH,
    )


def coef_kernel(
    density_ref,
    speed_ref,
    flags_ref,
    mass_ref,
    eigs_ref,
    send_ref,
    face_ref,
    fcol_ref,
    coef_ref,
    outgoing,
    arrived,
    returning,
    back,
    top_out,
    tops,
    send_a,
    recv_a,
    send_b,
    recv_b,
    send_c,
    recv_c,
):
    me = lax.axis_index("dom")
    group = lax.axis_index("group")
    barrier = pltpu.get_barrier_semaphore()

    def greet(k, carry):
        pl.semaphore_signal(
            barrier, inc=1, device_id={"dom": lax.rem(me + k, N_DOM)}, device_id_type=MESH
        )
        return carry

    lax.fori_loop(1, N_DOM, greet, 0)

    def greet_group(k, carry):
        pl.semaphore_signal(
            barrier, inc=1, device_id={"group": lax.rem(group + k, N_GROUP)}, device_id_type=MESH
        )
        return carry

    lax.fori_loop(1, N_GROUP, greet_group, 0)

    speed = speed_ref[...]
    eps = element_eps(density_ref[...], speed, flags_ref[...])
    slots = send_ref[...]
    lane = iota((N_DOM, LANES), 1)
    values = jnp.take_along_axis(
        jnp.broadcast_to(eps, (N_DOM, LANES)), slots & (ELEM_DEV - 1), axis=1
    )
    values = jnp.where(slots < SLOTS, values, 0.0)
    values = jnp.where(lane == LANES - 1, jnp.max(speed, axis=1, keepdims=True), values)
    for q in range(N_DOM):
        outgoing[q] = values[q : q + 1, :]

    pl.semaphore_wait(barrier, N_DOM + N_GROUP - 2)

    def send_first(k, carry):
        q = lax.rem(me + k, N_DOM)
        remote(outgoing.at[q], arrived.at[me], send_a, recv_a, {"dom": q}).start()
        return carry

    lax.fori_loop(1, N_DOM, send_first, 0)
    arrived[me] = outgoing[me]
    partner_p, partner_i = partner_rows(face_ref, fcol_ref)
    others = pl.ds(0, N_DOM - 1)
    whole = remote(outgoing.at[others], arrived.at[others], send_a, recv_a, {"dom": lax.rem(me + 1, N_DOM)})
    whole.wait_recv()
    whole.wait_send()

    partner_eps = jnp.zeros((16, LANES), F32)
    top = jnp.zeros((1, LANES), F32)
    for p in range(N_DOM):
        row = arrived[p]
        top = jnp.maximum(top, row)
        found = jnp.take_along_axis(jnp.broadcast_to(row, (16, LANES)), partner_i, axis=1)
        partner_eps = jnp.where(partner_p == p, found, partner_eps)
    for r in range(16):
        returning[r] = partner_eps[r : r + 1, :]
    top_out[0] = top

    def send_second(k, carry):
        p = lax.rem(me + k, N_DOM)
        remote(returning.at[lax.div(p, 4)], back.at[me], send_b, recv_b, {"dom": p}).start()
        return carry

    lax.fori_loop(1, N_DOM, send_second, 0)

    def send_top(k, carry):
        other = lax.rem(group + k, N_GROUP)
        remote(top_out.at[0], tops.at[group], send_c, recv_c, {"group": other}).start()
        return carry

    lax.fori_loop(1, N_GROUP, send_top, 0)
    back[me] = returning[lax.div(me, 4)]
    tops[group] = top_out[0]

    whole = remote(arrived.at[others], back.at[others], send_b, recv_b, {"dom": lax.rem(me + 1, N_DOM)})
    whole.wait_recv()
    whole.wait_send()
    seven = pl.ds(0, N_GROUP - 1)
    whole = remote(tops.at[seven], tops.at[seven], send_c, recv_c, {"group": lax.rem(group + 1, N_GROUP)})
    whole.wait_recv()
    whole.wait_send()

    rows = jnp.concatenate([back[q] for q in range(N_DOM)], axis=0)
    rows = pltpu.roll(rows, lax.rem(4 - lax.rem(me, 4), 4) * 32, 1)
    total = jnp.zeros((N_DOM, LANES), F32)
    for i in range(CAP):
        slot = slots[:, i : i + 1]
        here = jnp.logical_and((slot & (ELEM_DEV - 1)) == lane, slot < SLOTS)
        total = total + jnp.where(here, rows[:, i : i + 1], 0.0)
    gathered = jnp.sum(total, axis=0, keepdims=True)
    nu = NU_BASE + (EFACES * eps + gathered) / (2.0 * EFACES)
    top = tops[0]
    for g in range(1, N_GROUP):
        top = jnp.maximum(top, tops[g])
    lane_one = iota((1, LANES), 1)
    peak = jnp.max(jnp.where(lane_one == LANES - 1, top, 0.0), axis=1, keepdims=True)
    coef_ref[...] = 1.0 / (mass_ref[...] * (1.0 + speed / peak + nu * eigs_ref[...]))


def coefficients(density, speed, flags, mass, eigs, send64, face_rows, fcols):
    vmem = pl.BlockSpec(memory_space=pltpu.VMEM)
    return pl.pallas_call(
        coef_kernel,
        out_shape=jax.ShapeDtypeStruct((MODES, LANES), F32),
        in_specs=[vmem] * 8,
        out_specs=vmem,
        scratch_shapes=[
            pltpu.VMEM((N_DOM, 1, LANES), F32),
            pltpu.VMEM((N_DOM, 1, LANES), F32),
            pltpu.VMEM((16, 1, LANES), F32),
            pltpu.VMEM((N_DOM, 1, LANES), F32),
            pltpu.VMEM((1, 1, LANES), F32),
            pltpu.VMEM((N_GROUP, 1, LANES), F32),
        ]
        + [pltpu.SemaphoreType.DMA] * 6,
        compiler_params=pltpu.CompilerParams(collective_id=0, has_side_effects=True),
        name="coefficients",
    )(density, speed, flags, mass, eigs, send64, face_rows, fcols)


def block_kernel(coef_ref, coupling_ref, inner_ref, face_ref, scol_ref, out_ref, tail_ref, pay, rows):
    for j in range(EFACES):
        def body(k, sums):
            coef = coef_ref[pl.ds(k, 1), :]
            c = coupling_ref[k, j * FNODES : (j + 1) * FNODES, :].astype(F32)
            u = c * coef
            new = [sums[0] + u * c]
            for d in range(1, 8):
                new.append(sums[d] + u * pltpu.roll(c, FNODES - d, 0))
            new.append(sums[8] + u[0:8] * c[8:16])
            for comp in range(COMPS):
                new.append(sums[9 + comp] + c * (coef * inner_ref[comp, pl.ds(k, 1), :]))
            return tuple(new)

        full = jnp.zeros((FNODES, LANES), F32)
        start = (full + TAU_STAB,) + (full,) * 7 + (jnp.zeros((8, LANES), F32),) + (full,) * COMPS
        sums = lax.fori_loop(0, MODES, body, start, unroll=2)
        at = pl.ds(j * LANES, LANES)
        for d in range(9):
            height = 16 if d < 8 else 8
            pay[pl.ds(d * 16, height), at] = sums[d]
        for comp in range(COMPS):
            pay[pl.ds(TRI + comp * FNODES, FNODES), at] = (
                face_ref[comp, j * FNODES : (j + 1) * FNODES, :] - sums[9 + comp]
            )
        pay[pl.ds(216, WIDE - 216), at] = jnp.zeros((WIDE - 216, LANES), F32)

    parts = split3(pay[...])
    lane = iota((8, LANES), 1)
    sub = iota((8, LANES), 0)
    for chunk in range(4):
        hot = one_hot(iota((384, SLOTS), 1) == scol_ref[:, chunk : chunk + 1])
        rows[...] = dot(hot, parts[0], NT) + dot(hot, parts[1], NT) + dot(hot, parts[2], NT)

        def pack(n, carry):
            q = chunk * 16 + n
            base = pl.multiple_of(n * CAP, 8)
            out_ref[q, 0:CAP, :] = rows[pl.ds(base, CAP), 0:LANES]
            x0 = rows[pl.ds(base, 8), LANES:WIDE]
            x1 = rows[pl.ds(base + 8, 8), LANES:WIDE]
            x2 = rows[pl.ds(base + 16, 8), LANES:WIDE]
            out_ref[q, CAP : CAP + 8, :] = jnp.where(lane < 64, x0, pltpu.roll(x1, 64, 1))
            out_ref[q, CAP + 8 : CAP + 16, :] = jnp.where(
                lane < 64,
                x2,
                jnp.where(
                    lane < 88,
                    x0,
                    jnp.where(lane < 112, pltpu.roll(x1, 24, 1), pltpu.roll(x2, 48, 1)),
                ),
            )
            spread = pltpu.roll(x2, 48, 1, stride=8, stride_axis=0)
            tail_ref[q] = jnp.sum(jnp.where((lane >> 3) == sub, spread, 0.0), axis=0, keepdims=True)
            return carry

        lax.fori_loop(0, 16, pack, 0)


def blocks_packed(coef, coupling, inner, face_res, scol):
    vmem = pl.BlockSpec(memory_space=pltpu.VMEM)
    return pl.pallas_call(
        block_kernel,
        out_shape=(
            jax.ShapeDtypeStruct((N_DOM, OUT_TILE, LANES), F32),
            jax.ShapeDtypeStruct((N_DOM, 1, LANES), F32),
        ),
        in_specs=[vmem] * 5,
        out_specs=(vmem, vmem),
        scratch_shapes=[pltpu.VMEM((WIDE, SLOTS), F32), pltpu.VMEM((384, WIDE), F32)],
        compiler_params=pltpu.CompilerParams(vmem_limit_bytes=VMEM_LIMIT),
        name="blocks_packed",
    )(coef, coupling, inner, face_res, scol)


def exchange_kernel(count, *refs):
    sources = refs[:count]
    targets = refs[count : 2 * count]
    send_sem, recv_sem, own_sem = refs[2 * count :]
    me = lax.axis_index("dom")
    barrier = pltpu.get_barrier_semaphore()

    def greet(k, carry):
        pl.semaphore_signal(
            barrier, inc=1, device_id={"dom": lax.rem(me + k, N_DOM)}, device_id_type=MESH
        )
        return carry

    lax.fori_loop(1, N_DOM, greet, 0)
    own = [
        pltpu.make_async_copy(sources[n].at[me], targets[n].at[me], own_sem.at[n])
        for n in range(count)
    ]
    for copy in own:
        copy.start()
    pl.semaphore_wait(barrier, N_DOM - 1)

    def start(k, carry):
        q = lax.rem(me + k, N_DOM)
        for n in range(count):
            remote(
                sources[n].at[q], targets[n].at[me], send_sem.at[n], recv_sem.at[n], {"dom": q}
            ).start()
        return carry

    lax.fori_loop(1, N_DOM, start, 0)
    for copy in own:
        copy.wait()
    others = pl.ds(0, N_DOM - 1)
    for n in range(count):
        whole = remote(
            sources[n].at[others],
            targets[n].at[others],
            send_sem.at[n],
            recv_sem.at[n],
            {"dom": lax.rem(me + 1, N_DOM)},
        )
        whole.wait_recv()
        whole.wait_send()


def exchange(arrays, collective_id):
    anywhere = pl.BlockSpec(memory_space=pl.ANY)
    count = len(arrays)
    return pl.pallas_call(
        functools.partial(exchange_kernel, count),
        out_shape=tuple(jax.ShapeDtypeStruct(a.shape, a.dtype) for a in arrays),
        in_specs=[anywhere] * count,
        out_specs=(anywhere,) * count,
        scratch_shapes=[pltpu.SemaphoreType.DMA((count,))] * 3,
        compiler_params=pltpu.CompilerParams(collective_id=collective_id, has_side_effects=True),
        name=f"exchange_{collective_id}",
    )(*arrays)


def solve_faces(grid, idle):
    def entry(i, j):
        d = (j - i) % FNODES
        if d > 8 or (d == 8 and i >= 8):
            i, d = j, FNODES - d
        return grid(d * 16 + i)

    scaled = [[None] * FNODES for _ in range(FNODES)]
    lower = [[None] * FNODES for _ in range(FNODES)]
    inverse = [None] * FNODES
    for j in range(FNODES):
        for i in range(j, FNODES):
            total = entry(i, j)
            if i == j:
                total = total + idle
            for k in range(j):
                total = total - scaled[i][k] * lower[j][k]
            if i == j:
                inverse[j] = 1.0 / total
            else:
                scaled[i][j] = total
                lower[i][j] = total * inverse[j]
    solved = [[None] * FNODES for _ in range(COMPS)]
    for comp in range(COMPS):
        forward = []
        for i in range(FNODES):
            total = grid(TRI + comp * FNODES + i)
            for k in range(i):
                total = total - lower[i][k] * forward[k]
            forward.append(total)
        for i in reversed(range(FNODES)):
            total = forward[i] * inverse[i]
            for k in range(i + 1, FNODES):
                total = total - lower[k][i] * solved[comp][k]
            solved[comp][i] = total
    return solved


def solve_kernel(arrived_ref, tail_ref, face_ref, fcol_ref, idle_ref, ret_ref, part_a, part_b, part_c, grid, answer, rows):
    lane = iota((8, LANES), 1)
    sub = iota((8, LANES), 0)

    def unpack(p, carry):
        base = pl.multiple_of(p * CAP, 8)
        b = arrived_ref[p, CAP : CAP + 8, :]
        c = arrived_ref[p, CAP + 8 : CAP + 16, :]
        tail = jnp.broadcast_to(tail_ref[p], (8, LANES))
        spread = jnp.take_along_axis(
            pltpu.roll(tail, 24, 1, stride=8, stride_axis=0), 7 - sub, axis=0
        )
        zero = jnp.zeros((8, LANES), F32)
        x0 = jnp.where(lane < 64, b, jnp.where(lane < 88, c, zero))
        x1 = jnp.where(
            lane < 64, pltpu.roll(b, 64, 1), jnp.where(lane < 88, pltpu.roll(c, 104, 1), zero)
        )
        x2 = jnp.where(
            lane < 64,
            c,
            jnp.where(lane < 80, pltpu.roll(c, 80, 1), jnp.where(lane < 88, spread, zero)),
        )
        rows[pl.ds(base, CAP), 0:LANES] = arrived_ref[p, 0:CAP, :]
        rows[pl.ds(base, 8), LANES:WIDE] = x0
        rows[pl.ds(base + 8, 8), LANES:WIDE] = x1
        rows[pl.ds(base + 16, 8), LANES:WIDE] = x2
        return carry

    lax.fori_loop(0, N_DOM, unpack, 0, unroll=2)
    high, middle, low = split3(rows[...])
    part_a[...] = high
    part_b[...] = middle
    part_c[...] = low
    for chunk in range(6):
        first = fcol_ref[:, chunk : chunk + 1]
        second = fcol_ref[:, 6 + chunk : 7 + chunk]
        received = iota((LANES, ROWS), 1)
        hot = one_hot(jnp.logical_or(received == first, received == second))
        joined = (
            dot(hot, part_a[...], NN) + dot(hot, part_b[...], NN) + dot(hot, part_c[...], NN)
        )
        turned = jnp.transpose(joined)
        grid[pl.ds(chunk, 216, stride=8), :] = turned[0:216, :]

    solved = solve_faces(lambda n: grid[n * 8 : n * 8 + 8, :], idle_ref[...])
    for comp in range(COMPS):
        for i in range(FNODES):
            n = comp * FNODES + i
            answer[n * 8 : n * 8 + 8, :] = solved[comp][i]
    traces = jnp.concatenate(
        [answer[pl.ds(chunk, COMPS * FNODES, stride=8), :] for chunk in range(6)], axis=1
    )
    gap = jnp.zeros((LANES - COMPS * FNODES, FACES), BF16)
    high, low = split2(traces)
    both = jnp.concatenate([high, gap, low, gap], axis=0)
    for chunk in range(4):
        received = iota((384, FACES), 0) + chunk * 384
        hot = one_hot(
            jnp.logical_or(received == face_ref[0:1, :], received == face_ref[1:2, :])
        )
        found = dot(hot, both, NT)
        rows[pl.ds(chunk * 384, 384), 0:LANES] = found[:, 0:LANES] + found[:, LANES:WIDE]

    def pack(p, carry):
        base = pl.multiple_of(p * CAP, 8)
        y0 = rows[pl.ds(base, 8), 0:LANES]
        y1 = rows[pl.ds(base + 8, 8), 0:LANES]
        y2 = rows[pl.ds(base + 16, 8), 0:LANES]
        ret_ref[p, 0:8, :] = jnp.where(lane < 64, y0, pltpu.roll(y1, 64, 1))
        ret_ref[p, 8:16, :] = jnp.where(
            lane < 64,
            y2,
            jnp.where(
                lane < 80, y0, jnp.where(lane < 96, pltpu.roll(y1, 16, 1), pltpu.roll(y2, 32, 1))
            ),
        )
        return carry

    lax.fori_loop(0, N_DOM, pack, 0, unroll=2)


def face_traces(arrived, tails, face_rows, fcols, idle):
    vmem = pl.BlockSpec(memory_space=pltpu.VMEM)
    return pl.pallas_call(
        solve_kernel,
        out_shape=jax.ShapeDtypeStruct((N_DOM, RET_TILE, LANES), F32),
        in_specs=[vmem] * 5,
        out_specs=vmem,
        scratch_shapes=[
            pltpu.VMEM((ROWS, WIDE), BF16),
            pltpu.VMEM((ROWS, WIDE), BF16),
            pltpu.VMEM((ROWS, WIDE), BF16),
            pltpu.VMEM((216 * 8, LANES), F32),
            pltpu.VMEM((80 * 8, LANES), F32),
            pltpu.VMEM((ROWS, WIDE), F32),
        ],
        compiler_params=pltpu.CompilerParams(vmem_limit_bytes=VMEM_LIMIT),
        name="face_traces",
    )(arrived, tails, face_rows, fcols, idle)


def update_kernel(back_ref, srow_ref, coef_ref, coupling_ref, inner_ref, update_ref, traces_ref, parts):
    lane = iota((8, LANES), 1)

    def unpack(q, carry):
        base = pl.multiple_of(q * CAP, 8)
        b = back_ref[q, 0:8, :]
        c = back_ref[q, 8:16, :]
        zero = jnp.zeros((8, LANES), F32)
        y0 = jnp.where(lane < 64, b, jnp.where(lane < 80, c, zero))
        y1 = jnp.where(
            lane < 64, pltpu.roll(b, 64, 1), jnp.where(lane < 80, pltpu.roll(c, 112, 1), zero)
        )
        y2 = jnp.where(lane < 64, c, jnp.where(lane < 80, pltpu.roll(c, 96, 1), zero))
        parts[pl.ds(base, CAP), :] = jnp.concatenate([y0, y1, y2], axis=0)
        return carry

    lax.fori_loop(0, N_DOM, unpack, 0, unroll=2)
    high, low = split2(parts[...])
    both = jnp.concatenate([high, low], axis=1)
    for j in range(EFACES):
        slot = iota((LANES, ROWS), 0) + j * LANES
        hot = one_hot(slot == srow_ref[...])
        found = dot(hot, both, NN)
        turned = jnp.transpose(found[:, 0:LANES] + found[:, LANES:WIDE])
        for comp in range(COMPS):
            traces_ref[comp, j * FNODES : (j + 1) * FNODES, :] = turned[
                comp * FNODES : (comp + 1) * FNODES, :
            ]

    def body(k, carry):
        c = coupling_ref[k].astype(F32)
        coef = coef_ref[pl.ds(k, 1), :]
        for comp in range(COMPS):
            pulled = jnp.sum(c * traces_ref[comp], axis=0, keepdims=True)
            update_ref[comp, pl.ds(k, 1), :] = coef * (inner_ref[comp, pl.ds(k, 1), :] - pulled)
        return carry

    lax.fori_loop(0, MODES, body, 0, unroll=2)


def back_substitute(back, srow, coef, coupling, inner):
    vmem = pl.BlockSpec(memory_space=pltpu.VMEM)
    return pl.pallas_call(
        update_kernel,
        out_shape=(
            jax.ShapeDtypeStruct((COMPS, MODES, LANES), F32),
            jax.ShapeDtypeStruct((COMPS, TRACE, LANES), F32),
        ),
        in_specs=[vmem] * 5,
        out_specs=(vmem, vmem),
        scratch_shapes=[pltpu.VMEM((ROWS, LANES), F32)],
        compiler_params=pltpu.CompilerParams(vmem_limit_bytes=VMEM_LIMIT),
        name="back_substitute",
    )(back, srow, coef, coupling, inner)


def local(
    density_modes,
    wave_speed,
    shock_flags,
    elem_mass,
    stiff_eigs,
    coupling,
    interior_res,
    face_res,
    send_rows,
    face_rows,
):
    send64 = jnp.pad(
        send_rows.reshape(N_DOM, CAP), ((0, 0), (0, LANES - CAP)), constant_values=SLOTS
    )
    scol = send_rows.reshape(4, 384).T
    fcols = face_rows.reshape(12, LANES).T
    idle = jnp.where(
        jnp.concatenate(
            [face_rows[0].reshape(6, LANES), jnp.full((2, LANES), ROWS, I32)], axis=0
        )
        < ROWS,
        0.0,
        1.0,
    ).astype(F32)
    coef = coefficients(
        density_modes,
        wave_speed[None, :],
        shock_flags[None, :],
        elem_mass[None, :],
        stiff_eigs[:, None],
        send64,
        face_rows,
        fcols,
    )
    packed, tails = blocks_packed(coef, coupling, interior_res, face_res, scol)
    arrived, arrived_tails = exchange((packed, tails), 1)
    returning = face_traces(arrived, arrived_tails, face_rows, fcols, idle)
    (back,) = exchange((returning,), 2)
    return back_substitute(back, send_rows[None, :], coef, coupling, interior_res)


def solution(mesh):
    return jax.shard_map(
        local,
        mesh=mesh,
        in_specs=(
            P(None, ("group", "dom")),
            P(("group", "dom")),
            P(("group", "dom")),
            P(("group", "dom")),
            P(),
            P(None, None, ("group", "dom")),
            P(None, None, ("group", "dom")),
            P(None, None, ("group", "dom")),
            P(("group", "dom")),
            P(None, ("group", "dom")),
        ),
        out_specs=(P(None, None, ("group", "dom")), P(None, None, ("group", "dom"))),
        check_vma=False,
    )
```

time: 429 us -> 182 us (0.42)
  Pallas kernels: 0 us -> 172 us
  blocking collectives: 158 us -> 0 us
  waiting for transfers between devices: 109 us -> 0 us
  local copies, waits for them, and re-layouts: 79.9 us -> 6.34 us
  starting transfers between devices: 40.1 us -> 0 us
  other arithmetic: 24.2 us -> 0.6 us
  matrix products: 14.8 us -> 0 us
    pallas_call x0 -> x6, Pallas kernels: none -> 172 us  [the longest x2 99.3 us: exchange(): pl.pallas_call(functools.partial(exchange_kernel, count), out_shape=tuple...]
    all_to_all x3 -> x0, waiting for transfers between devices: 109 us -> none  [the longest x1 108 us: local(): lax.all_to_all(outgoing_blocks, 'dom', split_axis=0, concat_axis=0, tiled...]
    pmax x1 -> x0, blocking collectives: 108 us -> none  [local(): peak = lax.pmax(jnp.max(wave_speed), ('group', 'dom'))]
    all_to_all x1 -> x0, blocking collectives: 50.2 us -> none  [local(): lax.all_to_all(returning_traces, 'dom', split_axis=0, concat_axis=0, tile...]
    all_to_all x3 -> x0, starting transfers between devices: 40.1 us -> none  [the longest x1 15.1 us: local(): lax.all_to_all(returning, 'dom', split_axis=0, concat_axis=0, tiled=True)]
    gather x10 -> x0, local copies, waits for them, and re-layouts: 38.1 us -> none  [the longest x2 8.93 us: local(): face_visc = 0.5 * (arrived[first_clip] + arrived[second_clip])]
    dot_general x3 -> x0, matrix products: 14.8 us -> none  [the longest x1 8.66 us: element_terms(): jnp.einsum('kjan,kjbn->jabn', shaped_scaled, shaped_full, precision=lax.P...]
    scatter x3 -> x0, local copies, waits for them, and re-layouts: 13 us -> none  [the longest x2 6.78 us: local(): row_face = jnp.full((row_total,), face_total, jnp.int32).at[first_row].se...]
  transfers between devices with their start and end apart: 3 -> 0, of which waited for: 2 -> 0; matrix products, arithmetic and copies ran while one was open for 6% -> 0% of each run, Pallas kernels for 0% -> 0%
where the time goes in v1:
time: 182 us; the launch traced here: 180 us
  Pallas kernels  172 us (95%)
  local copies, waits for them, and re-layouts  6.34 us (3%)
    pallas_call x2, Pallas kernels, exchange(): pl.pallas_call(functools.partial(exchange_kernel, count), out_shape=tuple...  99.3 us
    pallas_call x1, Pallas kernels, coefficients(): pl.pallas_call(coef_kernel, out_shape=jax.ShapeDtypeStruct((MODES, LANES)...  35.1 us
    pallas_call x1, Pallas kernels, blocks_packed(): pl.pallas_call(block_kernel, out_shape=(jax.ShapeDtypeStruct((N_DOM, OUT_...  18.8 us
    pallas_call x1, Pallas kernels, face_traces(): pl.pallas_call(solve_kernel, out_shape=jax.ShapeDtypeStruct((N_DOM, RET_T...  11.6 us
    pallas_call x1, Pallas kernels, back_substitute(): pl.pallas_call(update_kernel, out_shape=(jax.ShapeDtypeStruct((COMPS, MOD...  7.35 us

profile of v1, /device:TPU:24, one launch (start us, length us, event | category | flops | bytes accessed | tf_op | source)
XLA Modules:
  0.0 179.8 jit_solution(4935196466117357431)
XLA Ops:
  0.6 0.7 reshape.14
  1.3 0.7 copy.13
  2.1 0.8 reshape.13
  2.9 0.6 pad.5.send_ref
  3.5 1.4 copy.14.eigs_ref
  4.8 35.1 %coefficients.1.coef_ref = f32[64,128]{1,0:T(8,128)} custom-call(f32[64,128]{1,0:T(8,128)} %density_ref.1, f32[1,128]{1,0:T(1,128)} %bitcast.12, s32[1,128]{1,0:T(1,128)} %bitcast.13, f32[1,128]{1,0:T(1,128)} %bitcast.14, f32[64,1]{1,0:T(8,128)} %copy.14.eigs_ref, s32[64,128]{1,0:T(8,128)} %pad.5.send_ref, s32[2,768]{1,0:T(2,128)} %face_ref.5, s32[128,12]{1,0:T(8,128)} %bitcast.8), custom_call_target="tpu_custom_call" | custom-call | tf_op jit(solution)/shard_map/coefficients/pallas_call | solution.py:247
  39.9 0.7 reshape.15
  40.7 0.8 copy.15
  41.5 0.0 copy-start
  41.5 18.8 %blocks_packed.1 = (f32[64,40,128]{2,1,0:T(8,128)}, f32[64,1,128]{2,1,0:T(1,128)}) custom-call(f32[64,128]{1,0:T(8,128)} %coefficients.1.coef_ref, bf16[64,96,128]{2,1,0:T(8,128)(2,1)} %coupling_ref.3, f32[5,64,128]{2,1,0:T(8,128)} %inner_ref.3, f32[5,96,128]{2,1,0:T(8,128)} %face_ref.4, s32[384,4]{1,0:T(8,128)} %bitcast.7), custom_call_target="tpu_custom_call" | custom-call | tf_op jit(solution)/shard_map/blocks_packed/pallas_call | solution.py:326
  60.3 68.9 %exchange_1.1 = (f32[64,40,128]{2,1,0:T(8,128)}, f32[64,1,128]{2,1,0:T(1,128)}) custom-call(f32[64,40,128]{2,1,0:T(8,128)} %get-tuple-element.6.refs_0_, f32[64,1,128]{2,1,0:T(1,128)} %get-tuple-element.7.refs_1_), custom_call_target="tpu_custom_call" | custom-call | tf_op jit(solution)/shard_map/exchange_1/pallas_call | solution.py:389
  129.1 0.0 copy-done
  129.2 0.6 fusion.idle_ref
  129.8 0.0 copy-start.1
  129.8 11.6 %face_traces.1.refs_0_ = f32[64,16,128]{2,1,0:T(8,128)} custom-call(f32[64,40,128]{2,1,0:T(8,128)} %get-tuple-element.8.arrived_ref, f32[64,1,128]{2,1,0:T(1,128)} %get-tuple-element.9.tail_ref, s32[2,768]{1,0:T(2,128)} %face_ref.5, s32[128,12]{1,0:T(8,128)} %bitcast.9, f32[8,128]{1,0:T(8,128)} %fusion.idle_ref), custom_call_target="tpu_custom_call" | custom-call | tf_op jit(solution)/shard_map/face_traces/pallas_call | solution.py:521
  141.4 30.5 %exchange_2.1.back_ref = f32[64,16,128]{2,1,0:T(8,128)} custom-call(f32[64,16,128]{2,1,0:T(8,128)} %face_traces.1.refs_0_), custom_call_target="tpu_custom_call" | custom-call | tf_op jit(solution)/shard_map/exchange_2/pallas_call | solution.py:389
  171.9 0.0 copy-done.1
  171.9 0.6 broadcast_in_dim.30.srow_ref
  172.5 7.3 %back_substitute.1 = (f32[5,64,128]{2,1,0:T(8,128)}, f32[5,96,128]{2,1,0:T(8,128)}) custom-call(f32[64,16,128]{2,1,0:T(8,128)} %exchange_2.1.back_ref, s32[1,1536]{1,0:T(1,128)} %broadcast_in_dim.30.srow_ref, f32[64,128]{1,0:T(8,128)} %coefficients.1.coef_ref, bf16[64,96,128]{2,1,0:T(8,128)(2,1)} %coupling_ref.3, f32[5,64,128]{2,1,0:T(8,128)} %inner_ref.3), custom_call_target="tpu_custom_call" | custom-call | tf_op jit(solution)/shard_map/back_substitute/pallas_call | solution.py:581
  (1 shorter events, 0.0 us)
Async XLA Ops:
  41.5 87.6 %copy-start = (s32[2,768]{1,0:T(2,128)S(1)}, s32[2,768]{1,0:T(2,128)}, u32[]{:S(2)}) copy-start(s32[2,768]{1,0:T(2,128)} %face_ref.5) | copy-start | bytes 18436
  129.8 42.1 %copy-start.1 = (s32[1536]{0:T(1024)S(1)}, s32[1536]{0:T(1024)}, u32[]{:S(2)}) copy-start(s32[1536]{0:T(1024)} %param.18) | copy-start | bytes 18436

commit v2 on v0

v2 whole, which is shorter than its diff:
```python
import jax
import jax.numpy as jnp
from jax import lax
from jax.experimental import pallas as pl
from jax.experimental.pallas import tpu as pltpu
from jax.sharding import PartitionSpec as P

MODES = 64
FNODES = 16
COMPS = 5
EFACES = 6
TRACE = 96
ELEM_DEV = 128
SLOTS = EFACES * ELEM_DEV
CAP = 24
N_DOM = 64
N_GROUP = 8
ROWS = N_DOM * CAP
FACES = 768
TRI = 136
USED = 216
HEIGHT = 224
WIDE = 256
N_Z = 16
N_Y = N_DOM // N_Z
PART = N_Z * CAP
LANES = 128
OUT_TILE = 40
RET_TILE = 16

EPS_SCALE = 0.1
NU_BASE = 0.02
TAU_STAB = 1.0
SENSOR_MID = -2.0
SENSOR_WIDTH = 0.5
RATIO_FLOOR = 0.0001

F32 = jnp.float32
BF16 = jnp.bfloat16
I32 = jnp.int32
MESH = pl.DeviceIdType.MESH
NN = (((1,), (0,)), ((), ()))
NT = (((1,), (1,)), ((), ()))
VMEM_LIMIT = 60 * 1024 * 1024


def iota(shape, axis):
    return lax.broadcasted_iota(I32, shape, axis)


def split3(x):
    high = x.astype(BF16)
    rest = x - high.astype(F32)
    middle = rest.astype(BF16)
    low = (rest - middle.astype(F32)).astype(BF16)
    return high, middle, low


def split2(x):
    high = x.astype(BF16)
    return high, (x - high.astype(F32)).astype(BF16)


def dot(a, b, dims):
    return lax.dot_general(a, b, dims, preferred_element_type=F32)


def one_hot(mask):
    return jnp.where(mask, 1.0, 0.0).astype(BF16)


def element_eps(density, speed, flags):
    ids = iota((MODES, LANES), 0)
    degree = jnp.maximum(jnp.maximum(ids >> 4, (ids >> 2) & 3), ids & 3)
    squares = density * density
    totals = jnp.sum(squares, axis=0, keepdims=True) + 1e-06
    high = jnp.sum(jnp.where(degree == 3, squares, 0.0), axis=0, keepdims=True)
    sensor = jnp.log10(jnp.maximum(high / totals, RATIO_FLOOR))
    ramped = 0.5 * (1.0 + jnp.tanh((sensor - SENSOR_MID) / SENSOR_WIDTH))
    return EPS_SCALE * speed * jnp.maximum(ramped, 0.5 * flags.astype(F32))


def padded_row(row):
    source = (row * 2731) >> 16
    return source, row - source * CAP


def partner_rows(face_ref):
    pieces = [
        face_ref[end : end + 1, chunk * LANES : (chunk + 1) * LANES]
        for end in range(2)
        for chunk in range(6)
    ]
    stacked = jnp.concatenate(pieces + [jnp.zeros((LANES - 12, LANES), I32)], axis=0)
    turned = jnp.transpose(stacked.astype(F32)).astype(I32)
    high_parts = []
    low_parts = []
    for end in range(2):
        own_p, own_i = padded_row(face_ref[end : end + 1, :])
        other_p, other_i = padded_row(face_ref[1 - end : 2 - end, :])
        mine = iota((16, FACES), 0) == (own_p >> 2)
        high_parts.append(
            jnp.concatenate(
                [
                    jnp.where(mine, other_p.astype(F32), 0.0),
                    jnp.where(mine, other_i.astype(F32), 0.0),
                ],
                axis=0,
            ).astype(BF16)
        )
        columns = []
        for chunk in range(6):
            n = end * 6 + chunk
            col_p, col_i = padded_row(turned[:, n : n + 1])
            place = ((col_p & 3) << 5) + col_i
            columns.append(one_hot(iota((LANES, LANES), 1) == place))
        low_parts.append(jnp.concatenate(columns, axis=0))
    found = dot(high_parts[0], low_parts[0], NN) + dot(high_parts[1], low_parts[1], NN)
    found = found.astype(I32)
    return found[0:16], found[16:32]


def remote(src, dst, send_sem, recv_sem, where):
    return pltpu.make_async_remote_copy(
        src_ref=src,
        dst_ref=dst,
        send_sem=send_sem,
        recv_sem=recv_sem,
        device_id=where,
        device_id_type=MESH,
    )


def condense(coef_ref, coupling_ref, inner_ref, face_ref, pay):
    for j in range(EFACES):

        def body(k, sums):
            coef = coef_ref[pl.ds(k, 1), :]
            c = coupling_ref[k, j * FNODES : (j + 1) * FNODES, :].astype(F32)
            u = c * coef
            new = [sums[0] + u * c]
            for d in range(1, 8):
                new.append(sums[d] + u * pltpu.roll(c, FNODES - d, 0))
            new.append(sums[8] + u[0:8] * c[8:16])
            for comp in range(COMPS):
                new.append(sums[9 + comp] + c * (coef * inner_ref[comp, pl.ds(k, 1), :]))
            return tuple(new)

        full = jnp.zeros((FNODES, LANES), F32)
        start = (full + TAU_STAB,) + (full,) * 7 + (jnp.zeros((8, LANES), F32),) + (full,) * COMPS
        sums = lax.fori_loop(0, MODES, body, start, unroll=2)
        at = pl.ds(j * LANES, LANES)
        for d in range(9):
            pay[pl.ds(d * 16, 16 if d < 8 else 8), at] = sums[d]
        for comp in range(COMPS):
            pay[pl.ds(TRI + comp * FNODES, FNODES), at] = (
                face_ref[comp, j * FNODES : (j + 1) * FNODES, :] - sums[9 + comp]
            )
        pay[pl.ds(USED, WIDE - USED), at] = jnp.zeros((WIDE - USED, LANES), F32)


def pack_blocks(rows, z, out_ref, tail_ref, q):
    lane = iota((8, LANES), 1)
    sub = iota((8, LANES), 0)
    mine = pl.ds(z, CAP, stride=16)
    rest = rows[1, mine, :]
    x0, x1, x2 = rest[0:8], rest[8:16], rest[16:24]
    out_ref[q, 0:CAP, :] = rows[0, mine, :]
    out_ref[q, CAP : CAP + 8, :] = jnp.where(lane < 64, x0, pltpu.roll(x1, 64, 1))
    out_ref[q, CAP + 8 : CAP + 16, :] = jnp.where(
        lane < 64,
        x2,
        jnp.where(
            lane < 88, x0, jnp.where(lane < 112, pltpu.roll(x1, 24, 1), pltpu.roll(x2, 48, 1))
        ),
    )
    spread = pltpu.roll(x2, 48, 1, stride=8, stride_axis=0)
    tail_ref[q] = jnp.sum(jnp.where((lane >> 3) == sub, spread, 0.0), axis=0, keepdims=True)


def unpack_blocks(arrived_ref, tail_ref, p, rows, z):
    lane = iota((8, LANES), 1)
    sub = iota((8, LANES), 0)
    b = arrived_ref[p, CAP : CAP + 8, :]
    c = arrived_ref[p, CAP + 8 : CAP + 16, :]
    tail = jnp.broadcast_to(tail_ref[p], (8, LANES))
    spread = jnp.take_along_axis(pltpu.roll(tail, 24, 1, stride=8, stride_axis=0), 7 - sub, axis=0)
    zero = jnp.zeros((8, LANES), F32)
    base = pl.multiple_of(z * CAP, 8)
    rows[0, pl.ds(base, CAP), :] = arrived_ref[p, 0:CAP, :]
    rows[1, pl.ds(base, 8), :] = jnp.where(lane < 64, b, jnp.where(lane < 88, c, zero))
    rows[1, pl.ds(base + 8, 8), :] = jnp.where(
        lane < 64, pltpu.roll(b, 64, 1), jnp.where(lane < 88, pltpu.roll(c, 104, 1), zero)
    )
    rows[1, pl.ds(base + 16, 8), :] = jnp.where(
        lane < 64,
        c,
        jnp.where(lane < 80, pltpu.roll(c, 80, 1), jnp.where(lane < 88, spread, zero)),
    )


def pack_traces(rows, z, ret_ref, p):
    lane = iota((8, LANES), 1)
    base = pl.multiple_of(z * CAP, 8)
    y0 = rows[0, pl.ds(base, 8), :]
    y1 = rows[0, pl.ds(base + 8, 8), :]
    y2 = rows[0, pl.ds(base + 16, 8), :]
    ret_ref[p, 0:8, :] = jnp.where(lane < 64, y0, pltpu.roll(y1, 64, 1))
    ret_ref[p, 8:16, :] = jnp.where(
        lane < 64,
        y2,
        jnp.where(lane < 80, y0, jnp.where(lane < 96, pltpu.roll(y1, 16, 1), pltpu.roll(y2, 32, 1))),
    )


def unpack_traces(back_ref, q, rows, z):
    lane = iota((8, LANES), 1)
    b = back_ref[q, 0:8, :]
    c = back_ref[q, 8:16, :]
    zero = jnp.zeros((8, LANES), F32)
    y0 = jnp.where(lane < 64, b, jnp.where(lane < 80, c, zero))
    y1 = jnp.where(
        lane < 64, pltpu.roll(b, 64, 1), jnp.where(lane < 80, pltpu.roll(c, 112, 1), zero)
    )
    y2 = jnp.where(lane < 64, c, jnp.where(lane < 80, pltpu.roll(c, 96, 1), zero))
    rows[0, pl.ds(z, CAP, stride=16), :] = jnp.concatenate([y0, y1, y2], axis=0)


def block_column(grid, j):
    entries = []
    for i in range(j, FNODES):
        d, s = i - j, j
        if d > 8 or (d == 8 and s >= 8):
            d, s = FNODES - d, i
        entries.append(grid[d * 16 + s])
    return jnp.stack(entries, axis=0)


def solve_faces(grid, idle):
    scaled = []
    lower = []
    inverse = []
    for j in range(FNODES):
        column = block_column(grid, j)
        for k in range(j):
            column = column - scaled[k][j - k :] * lower[k][j - k][None]
        pivot = 1.0 / (column[0] + idle)
        inverse.append(pivot)
        scaled.append(column)
        lower.append(column * pivot[None])
    forward = []
    for i in range(FNODES):
        total = jnp.stack([grid[TRI + comp * FNODES + i] for comp in range(COMPS)], axis=0)
        for k in range(i):
            total = total - lower[k][i - k][None] * forward[k]
        forward.append(total)
    solved = [None] * FNODES
    for i in reversed(range(FNODES)):
        total = forward[i] * inverse[i][None]
        for k in range(i + 1, FNODES):
            total = total - lower[i][k - i][None] * solved[k]
        solved[i] = total
    return solved


def ring_offset(t):
    half = lax.div(t + 1, 2)
    return lax.rem(16 + half * (2 * lax.rem(t, 2) - 1), 16)


def step_kernel(
    density_ref,
    speed_ref,
    flags_ref,
    mass_ref,
    eigs_ref,
    send_ref,
    face_ref,
    coupling_hbm,
    inner_hbm,
    faceres_hbm,
    update_ref,
    traces_ref,
    coupling,
    inner,
    faceres,
    coef_ref,
    eps_out,
    eps_in,
    visc_out,
    visc_in,
    top_out,
    tops,
    slot_hot,
    row_hot,
    pay,
    pay_parts,
    rows,
    packed,
    packed_tail,
    arrived,
    arrived_tail,
    joined,
    grid,
    answer,
    returning,
    back,
    load_sem,
    send_a,
    recv_a,
    send_b,
    recv_b,
    send_c,
    recv_c,
    send_d,
    recv_d,
    send_e,
    recv_e,
    send_f,
    recv_f,
):
    me = lax.axis_index("dom")
    group = lax.axis_index("group")
    my_y = lax.div(me, N_Z)
    my_z = lax.rem(me, N_Z)
    following = {"dom": lax.rem(me + 1, N_DOM)}
    barrier = pltpu.get_barrier_semaphore()

    def greet(k, carry):
        pl.semaphore_signal(
            barrier, inc=1, device_id={"dom": lax.rem(me + k, N_DOM)}, device_id_type=MESH
        )
        return carry

    lax.fori_loop(1, N_DOM, greet, 0)

    def greet_group(k, carry):
        pl.semaphore_signal(
            barrier, inc=1, device_id={"group": lax.rem(group + k, N_GROUP)}, device_id_type=MESH
        )
        return carry

    lax.fori_loop(1, N_GROUP, greet_group, 0)
    loads = [
        pltpu.make_async_copy(coupling_hbm, coupling, load_sem.at[0]),
        pltpu.make_async_copy(inner_hbm, inner, load_sem.at[1]),
        pltpu.make_async_copy(faceres_hbm, faceres, load_sem.at[2]),
    ]
    for copy in loads:
        copy.start()

    speed = speed_ref[...]
    eps = element_eps(density_ref[...], speed, flags_ref[...])
    slots = send_ref[...]
    slots = jnp.concatenate([slots, jnp.full((N_DOM, LANES - CAP), SLOTS, I32)], axis=1)
    lane = iota((N_DOM, LANES), 1)
    values = jnp.take_along_axis(
        jnp.broadcast_to(eps, (N_DOM, LANES)), slots & (ELEM_DEV - 1), axis=1
    )
    values = jnp.where(slots < SLOTS, values, 0.0)
    values = jnp.where(lane == LANES - 1, jnp.max(speed, axis=1, keepdims=True), values)
    for q in range(N_DOM):
        eps_out[q] = values[q : q + 1, :]

    for y in range(N_Y):
        for i in range(CAP):
            column = slots[y * N_Z : (y + 1) * N_Z, i : i + 1]
            slot_hot[y, i * N_Z : (i + 1) * N_Z, :] = one_hot(iota((N_Z, SLOTS), 1) == column)

    pl.semaphore_wait(barrier, N_DOM + N_GROUP - 2)

    def send_first(k, carry):
        q = lax.rem(me + k, N_DOM)
        remote(eps_out.at[q], eps_in.at[me], send_a, recv_a, {"dom": q}).start()
        return carry

    lax.fori_loop(1, N_DOM, send_first, 0)
    eps_in[me] = eps_out[me]
    partner_p, partner_i = partner_rows(face_ref)
    others = pl.ds(0, N_DOM - 1)
    whole = remote(eps_out.at[others], eps_in.at[others], send_a, recv_a, following)
    whole.wait_recv()
    whole.wait_send()

    partner_eps = jnp.zeros((16, LANES), F32)
    top = jnp.zeros((1, LANES), F32)
    for p in range(N_DOM):
        row = eps_in[p]
        top = jnp.maximum(top, row)
        found = jnp.take_along_axis(jnp.broadcast_to(row, (16, LANES)), partner_i, axis=1)
        partner_eps = jnp.where(partner_p == p, found, partner_eps)
    for r in range(16):
        visc_out[r] = partner_eps[r : r + 1, :]
    top_out[0] = top

    def send_second(k, carry):
        p = lax.rem(me + k, N_DOM)
        remote(visc_out.at[lax.div(p, 4)], visc_in.at[me], send_b, recv_b, {"dom": p}).start()
        return carry

    lax.fori_loop(1, N_DOM, send_second, 0)

    def send_top(k, carry):
        other = lax.rem(group + k, N_GROUP)
        remote(top_out.at[0], tops.at[group], send_c, recv_c, {"group": other}).start()
        return carry

    lax.fori_loop(1, N_GROUP, send_top, 0)
    visc_in[me] = visc_out[lax.div(me, 4)]
    tops[group] = top_out[0]

    for y in range(N_Y):
        received = iota((PART, FACES), 0) + y * PART
        row_hot[y] = one_hot(
            jnp.logical_or(received == face_ref[0:1, :], received == face_ref[1:2, :])
        )
    for copy in loads:
        copy.wait()

    whole = remote(eps_in.at[others], visc_in.at[others], send_b, recv_b, following)
    whole.wait_recv()
    whole.wait_send()
    seven = pl.ds(0, N_GROUP - 1)
    whole = remote(
        tops.at[seven],
        tops.at[seven],
        send_c,
        recv_c,
        {"group": lax.rem(group + 1, N_GROUP)},
    )
    whole.wait_recv()
    whole.wait_send()

    came = jnp.concatenate([visc_in[q] for q in range(N_DOM)], axis=0)
    came = pltpu.roll(came, lax.rem(4 - lax.rem(me, 4), 4) * 32, 1)
    total = jnp.zeros((N_DOM, LANES), F32)
    for i in range(CAP):
        slot = slots[:, i : i + 1]
        here = jnp.logical_and((slot & (ELEM_DEV - 1)) == lane, slot < SLOTS)
        total = total + jnp.where(here, came[:, i : i + 1], 0.0)
    gathered = jnp.sum(total, axis=0, keepdims=True)
    nu = NU_BASE + (EFACES * eps + gathered) / (2.0 * EFACES)
    top = tops[0]
    for g in range(1, N_GROUP):
        top = jnp.maximum(top, tops[g])
    peak = jnp.max(
        jnp.where(iota((1, LANES), 1) == LANES - 1, top, 0.0), axis=1, keepdims=True
    )
    square = iota((MODES, MODES), 0) == iota((MODES, MODES), 1)
    eigs = jnp.sum(jnp.where(square, eigs_ref[...], 0.0), axis=1, keepdims=True)
    coef_ref[...] = 1.0 / (mass_ref[...] * (1.0 + speed / peak + nu * eigs))

    condense(coef_ref, coupling, inner, faceres, pay)
    for n, part in enumerate(split3(pay[...])):
        pay_parts[n] = part
    for c in range(N_Y):
        y = lax.rem(my_y + c, N_Y)
        hot = slot_hot[y]
        found = dot(hot, pay_parts[0], NT) + dot(hot, pay_parts[1], NT) + dot(hot, pay_parts[2], NT)
        rows[0] = found[:, 0:LANES]
        rows[1] = found[:, LANES:WIDE]

        def send_blocks(n, carry):
            z = lax.rem(my_z + ring_offset(N_Z - 1 - n), N_Z)
            q = y * N_Z + z
            pack_blocks(rows, z, packed, packed_tail, q)
            remote(packed.at[q], arrived.at[me], send_d, recv_d.at[c], {"dom": q}).start()
            remote(packed_tail.at[q], arrived_tail.at[me], send_e, recv_e.at[c], {"dom": q}).start()
            return carry

        lax.fori_loop(0, N_Z if c else N_Z - 1, send_blocks, 0)
        if c == 0:
            pack_blocks(rows, my_z, packed, packed_tail, me)
            arrived[me] = packed[me]
            arrived_tail[me] = packed_tail[me]

    for c in range(N_Y):
        y = lax.rem(my_y + N_Y - c, N_Y)
        sources = pl.ds(0, N_Z if c else N_Z - 1)
        remote(
            packed.at[sources], arrived.at[sources], send_d, recv_d.at[c], following
        ).wait_recv()
        remote(
            packed_tail.at[sources], arrived_tail.at[sources], send_e, recv_e.at[c], following
        ).wait_recv()

        def take_blocks(z, carry):
            unpack_blocks(arrived, arrived_tail, y * N_Z + z, rows, z)
            return carry

        lax.fori_loop(0, N_Z, take_blocks, 0, unroll=2)
        turned = jnp.concatenate(
            [jnp.transpose(rows[0]), jnp.transpose(rows[1])[0 : HEIGHT - LANES]], axis=0
        )
        stacked = jnp.concatenate(split3(turned), axis=0)
        found = dot(stacked, row_hot[y], NN)
        found = found[0:HEIGHT] + found[HEIGHT : 2 * HEIGHT] + found[2 * HEIGHT :]
        joined[...] = found if c == 0 else joined[...] + found
    remote(packed.at[others], arrived.at[others], send_d, recv_d.at[0], following).wait_send()
    remote(
        packed_tail.at[others], arrived_tail.at[others], send_e, recv_e.at[0], following
    ).wait_send()
    for chunk in range(6):
        for n in range(USED // 8):
            grid[n * 8 : n * 8 + 8, chunk, :] = joined[
                n * 8 : n * 8 + 8, chunk * LANES : (chunk + 1) * LANES
            ]
    first = face_ref[0:1, :]
    idle = jnp.concatenate(
        [first[:, chunk * LANES : (chunk + 1) * LANES] for chunk in range(6)]
        + [jnp.full((2, LANES), ROWS, I32)],
        axis=0,
    )
    idle = jnp.where(idle < ROWS, 0.0, 1.0)
    solved = solve_faces(grid, idle)
    for i in range(FNODES):
        for comp in range(COMPS):
            answer[comp * FNODES + i] = solved[i][comp]
    face_traces = jnp.concatenate([answer[:, chunk, :] for chunk in range(6)], axis=1)
    gap = jnp.zeros((LANES - COMPS * FNODES, FACES), BF16)
    high, low = split2(face_traces)
    both = jnp.concatenate([high, gap, low, gap], axis=0)

    for c in range(N_Y):
        y = lax.rem(my_y + c, N_Y)
        found = dot(row_hot[y], both, NT)
        rows[0] = found[:, 0:LANES] + found[:, LANES:WIDE]

        def send_traces(n, carry):
            z = lax.rem(my_z + ring_offset(N_Z - 1 - n), N_Z)
            p = y * N_Z + z
            pack_traces(rows, z, returning, p)
            remote(returning.at[p], back.at[me], send_f, recv_f.at[c], {"dom": p}).start()
            return carry

        lax.fori_loop(0, N_Z if c else N_Z - 1, send_traces, 0)
        if c == 0:
            pack_traces(rows, my_z, returning, me)
            back[me] = returning[me]

    for c in range(N_Y):
        y = lax.rem(my_y + N_Y - c, N_Y)
        sources = pl.ds(0, N_Z if c else N_Z - 1)
        remote(returning.at[sources], back.at[sources], send_f, recv_f.at[c], following).wait_recv()

        def take_traces(z, carry):
            unpack_traces(back, y * N_Z + z, rows, z)
            return carry

        lax.fori_loop(0, N_Z, take_traces, 0, unroll=2)
        turned = jnp.transpose(rows[0])[0 : COMPS * FNODES]
        stacked = jnp.concatenate(split2(turned), axis=0)
        found = dot(stacked, slot_hot[y], NN)
        found = found[0 : COMPS * FNODES] + found[COMPS * FNODES :]
        for comp in range(COMPS):
            for j in range(EFACES):
                piece = found[
                    comp * FNODES : (comp + 1) * FNODES, j * LANES : (j + 1) * LANES
                ]
                at = slice(j * FNODES, (j + 1) * FNODES)
                traces_ref[comp, at, :] = piece if c == 0 else traces_ref[comp, at, :] + piece
    remote(returning.at[others], back.at[others], send_f, recv_f.at[0], following).wait_send()

    def substitute(k, carry):
        c = coupling[k].astype(F32)
        coef = coef_ref[pl.ds(k, 1), :]
        for comp in range(COMPS):
            pulled = jnp.sum(c * traces_ref[comp], axis=0, keepdims=True)
            update_ref[comp, pl.ds(k, 1), :] = coef * (inner[comp, pl.ds(k, 1), :] - pulled)
        return carry

    lax.fori_loop(0, MODES, substitute, 0, unroll=2)


def local(
    density_modes,
    wave_speed,
    shock_flags,
    elem_mass,
    stiff_eigs,
    coupling,
    interior_res,
    face_res,
    send_rows,
    face_rows,
):
    vmem = pl.BlockSpec(memory_space=pltpu.VMEM)
    anywhere = pl.BlockSpec(memory_space=pl.ANY)
    dma = pltpu.SemaphoreType.DMA
    return pl.pallas_call(
        step_kernel,
        out_shape=(
            jax.ShapeDtypeStruct((COMPS, MODES, LANES), F32),
            jax.ShapeDtypeStruct((COMPS, TRACE, LANES), F32),
        ),
        in_specs=[vmem] * 7 + [anywhere] * 3,
        out_specs=(vmem, vmem),
        scratch_shapes=[
            pltpu.VMEM((MODES, TRACE, LANES), BF16),
            pltpu.VMEM((COMPS, MODES, LANES), F32),
            pltpu.VMEM((COMPS, TRACE, LANES), F32),
            pltpu.VMEM((MODES, LANES), F32),
            pltpu.VMEM((N_DOM, 1, LANES), F32),
            pltpu.VMEM((N_DOM, 1, LANES), F32),
            pltpu.VMEM((16, 1, LANES), F32),
            pltpu.VMEM((N_DOM, 1, LANES), F32),
            pltpu.VMEM((1, 1, LANES), F32),
            pltpu.VMEM((N_GROUP, 1, LANES), F32),
            pltpu.VMEM((N_Y, PART, SLOTS), BF16),
            pltpu.VMEM((N_Y, PART, FACES), BF16),
            pltpu.VMEM((WIDE, SLOTS), F32),
            pltpu.VMEM((3, WIDE, SLOTS), BF16),
            pltpu.VMEM((2, PART, LANES), F32),
            pltpu.VMEM((N_DOM, OUT_TILE, LANES), F32),
            pltpu.VMEM((N_DOM, 1, LANES), F32),
            pltpu.VMEM((N_DOM, OUT_TILE, LANES), F32),
            pltpu.VMEM((N_DOM, 1, LANES), F32),
            pltpu.VMEM((HEIGHT, FACES), F32),
            pltpu.VMEM((USED, 8, LANES), F32),
            pltpu.VMEM((COMPS * FNODES, 8, LANES), F32),
            pltpu.VMEM((N_DOM, RET_TILE, LANES), F32),
            pltpu.VMEM((N_DOM, RET_TILE, LANES), F32),
            dma((3,)),
            dma,
            dma,
            dma,
            dma,
            dma,
            dma,
            dma,
            dma((N_Y,)),
            dma,
            dma((N_Y,)),
            dma,
            dma((N_Y,)),
        ],
        compiler_params=pltpu.CompilerParams(
            collective_id=0, has_side_effects=True, vmem_limit_bytes=VMEM_LIMIT
        ),
        name="newton_step",
    )(
        density_modes,
        wave_speed[None, :],
        shock_flags[None, :],
        elem_mass[None, :],
        stiff_eigs[None, :],
        send_rows.reshape(N_DOM, CAP),
        face_rows,
        coupling,
        interior_res,
        face_res,
    )


def solution(mesh):
    return jax.shard_map(
        local,
        mesh=mesh,
        in_specs=(
            P(None, ("group", "dom")),
            P(("group", "dom")),
            P(("group", "dom")),
            P(("group", "dom")),
            P(),
            P(None, None, ("group", "dom")),
            P(None, None, ("group", "dom")),
            P(None, None, ("group", "dom")),
            P(("group", "dom")),
            P(None, ("group", "dom")),
        ),
        out_specs=(P(None, None, ("group", "dom")), P(None, None, ("group", "dom"))),
        check_vma=False,
    )
```

time: 429 us -> 140 us (0.33)
  blocking collectives: 158 us -> 0 us
  Pallas kernels: 0 us -> 133 us
  waiting for transfers between devices: 109 us -> 0 us
  local copies, waits for them, and re-layouts: 79.9 us -> 4.64 us
  starting transfers between devices: 40.1 us -> 0 us
  other arithmetic: 24.2 us -> 0 us
  matrix products: 14.8 us -> 0 us
    pallas_call x0 -> x1, Pallas kernels: none -> 133 us  [local(): pl.pallas_call(step_kernel, out_shape=(jax.ShapeDtypeStruct((COMPS, MODES...]
    all_to_all x3 -> x0, waiting for transfers between devices: 109 us -> none  [the longest x1 108 us: local(): lax.all_to_all(outgoing_blocks, 'dom', split_axis=0, concat_axis=0, tiled...]
    pmax x1 -> x0, blocking collectives: 108 us -> none  [local(): peak = lax.pmax(jnp.max(wave_speed), ('group', 'dom'))]
    all_to_all x1 -> x0, blocking collectives: 50.2 us -> none  [local(): lax.all_to_all(returning_traces, 'dom', split_axis=0, concat_axis=0, tile...]
    all_to_all x3 -> x0, starting transfers between devices: 40.1 us -> none  [the longest x1 15.1 us: local(): lax.all_to_all(returning, 'dom', split_axis=0, concat_axis=0, tiled=True)]
    gather x10 -> x0, local copies, waits for them, and re-layouts: 38.1 us -> none  [the longest x2 8.93 us: local(): face_visc = 0.5 * (arrived[first_clip] + arrived[second_clip])]
    dot_general x3 -> x0, matrix products: 14.8 us -> none  [the longest x1 8.66 us: element_terms(): jnp.einsum('kjan,kjbn->jabn', shaped_scaled, shaped_full, precision=lax.P...]
    reshape x7 -> x1, local copies, waits for them, and re-layouts: 14.8 us -> 1.39 us  [local(): send_rows.reshape(N_DOM, CAP)]
  transfers between devices with their start and end apart: 3 -> 0, of which waited for: 2 -> 0; matrix products, arithmetic and copies ran while one was open for 6% -> 0% of each run, Pallas kernels for 0% -> 0%
where the time goes in v2:
time: 140 us; the launch traced here: 138 us
  Pallas kernels  133 us (95%)
  local copies, waits for them, and re-layouts  4.64 us (3%)
    pallas_call x1, Pallas kernels, local(): pl.pallas_call(step_kernel, out_shape=(jax.ShapeDtypeStruct((COMPS, MODES...  133 us
    unnamed x2, local copies, waits for them, and re-layouts  3.25 us

profile of v2, /device:TPU:24, one launch (start us, length us, event | category | flops | bytes accessed | tf_op | source)
XLA Modules:
  0.0 138.3 jit_solution(15467489212011464314)
XLA Ops:
  0.6 1.4 %reshape.7.send_ref = s32[64,24]{1,0:T(8,128)} reshape(s32[1536]{0:T(1024)} %param.18) | data formatting | bytes 12288 | tf_op jit(solution)/shard_map/reshape | solution.py:647
  2.0 133.0 %newton_step.1 = (f32[5,64,128]{2,1,0:T(8,128)}, f32[5,96,128]{2,1,0:T(8,128)}) custom-call(f32[64,128]{1,0:T(8,128)} %density_ref.1, f32[1,128]{1,0:T(1,128)} %bitcast.4, s32[1,128]{1,0:T(1,128)} %bitcast.5, f32[1,128]{1,0:T(1,128)} %bitcast.6, f32[1,64]{1,0:T(1,128)} %bitcast.7, s32[64,24]{1,0:T(8,128)} %reshape.7.send_ref, s32[2,768]{1,0:T(2,128)} %face_ref.1, ...), custom_call_target="tpu_custom_call" | custom-call | tf_op jit(solution)/shard_map/newton_step/pallas_call | solution.py:590
  135.1 1.6 %copy.14 = f32[5,64,128]{2,1,0:T(8,128)} copy(f32[5,64,128]{2,1,0:T(8,128)} %get-tuple-element.4) | data formatting | bytes 327680
  136.6 1.7 %copy.15 = f32[5,96,128]{2,1,0:T(8,128)} copy(f32[5,96,128]{2,1,0:T(8,128)} %get-tuple-element.5) | data formatting | bytes 491520

commit v3 on v2

v3 whole, which is shorter than its diff:
```python
import jax
import jax.numpy as jnp
from jax import lax
from jax.experimental import pallas as pl
from jax.experimental.pallas import tpu as pltpu
from jax.sharding import PartitionSpec as P

MODES = 64
FNODES = 16
COMPS = 5
EFACES = 6
TRACE = 96
ELEM_DEV = 128
SLOTS = EFACES * ELEM_DEV
CAP = 24
N_DOM = 64
N_GROUP = 8
ROWS = N_DOM * CAP
FACES = 768
TRI = 136
USED = 216
N_Z = 16
N_Y = N_DOM // N_Z
PART = N_Z * CAP
LANES = 128
HALF = 96
REST_TILE = 17
RET_TILE = 15

EPS_SCALE = 0.1
NU_BASE = 0.02
TAU_STAB = 1.0
SENSOR_MID = -2.0
SENSOR_WIDTH = 0.5
RATIO_FLOOR = 0.0001

F32 = jnp.float32
BF16 = jnp.bfloat16
I32 = jnp.int32
MESH = pl.DeviceIdType.MESH
NN = (((1,), (0,)), ((), ()))
NT = (((1,), (1,)), ((), ()))
VMEM_LIMIT = 60 * 1024 * 1024


def iota(shape, axis):
    return lax.broadcasted_iota(I32, shape, axis)


def split3(x):
    high = x.astype(BF16)
    rest = x - high.astype(F32)
    middle = rest.astype(BF16)
    low = (rest - middle.astype(F32)).astype(BF16)
    return high, middle, low


def split2(x):
    high = x.astype(BF16)
    return high, (x - high.astype(F32)).astype(BF16)


def dot(a, b, dims):
    return lax.dot_general(a, b, dims, preferred_element_type=F32)


def one_hot(mask):
    return jnp.where(mask, 1.0, 0.0).astype(BF16)


def element_eps(density, speed, flags):
    ids = iota((MODES, LANES), 0)
    degree = jnp.maximum(jnp.maximum(ids >> 4, (ids >> 2) & 3), ids & 3)
    squares = density * density
    totals = jnp.sum(squares, axis=0, keepdims=True) + 1e-06
    high = jnp.sum(jnp.where(degree == 3, squares, 0.0), axis=0, keepdims=True)
    sensor = jnp.log10(jnp.maximum(high / totals, RATIO_FLOOR))
    ramped = 0.5 * (1.0 + jnp.tanh((sensor - SENSOR_MID) / SENSOR_WIDTH))
    return EPS_SCALE * speed * jnp.maximum(ramped, 0.5 * flags.astype(F32))


def padded_row(row):
    source = (row * 2731) >> 16
    return source, row - source * CAP


def partner_rows(face_ref):
    pieces = [
        face_ref[end : end + 1, chunk * LANES : (chunk + 1) * LANES]
        for end in range(2)
        for chunk in range(6)
    ]
    stacked = jnp.concatenate(pieces + [jnp.zeros((LANES - 12, LANES), I32)], axis=0)
    turned = jnp.transpose(stacked.astype(F32)).astype(I32)
    high_parts = []
    low_parts = []
    for end in range(2):
        own_p, own_i = padded_row(face_ref[end : end + 1, :])
        other_p, other_i = padded_row(face_ref[1 - end : 2 - end, :])
        mine = iota((16, FACES), 0) == (own_p >> 2)
        high_parts.append(
            jnp.concatenate(
                [
                    jnp.where(mine, other_p.astype(F32), 0.0),
                    jnp.where(mine, other_i.astype(F32), 0.0),
                ],
                axis=0,
            ).astype(BF16)
        )
        columns = []
        for chunk in range(6):
            n = end * 6 + chunk
            col_p, col_i = padded_row(turned[:, n : n + 1])
            place = ((col_p & 3) << 5) + col_i
            columns.append(one_hot(iota((LANES, LANES), 1) == place))
        low_parts.append(jnp.concatenate(columns, axis=0))
    found = dot(high_parts[0], low_parts[0], NN) + dot(high_parts[1], low_parts[1], NN)
    found = found.astype(I32)
    return found[0:16], found[16:32]


def remote(src, dst, send_sem, recv_sem, where):
    return pltpu.make_async_remote_copy(
        src_ref=src,
        dst_ref=dst,
        send_sem=send_sem,
        recv_sem=recv_sem,
        device_id=where,
        device_id_type=MESH,
    )


def block_row(i, j):
    d = (i - j) % 8
    if i >= 8 > j:
        return 64 + d * 8 + j
    base = 32 if j >= 8 else 0
    low, high = j % 8, i % 8
    if d < 4:
        return base + d * 8 + low
    if d > 4:
        return base + (8 - d) * 8 + high
    return 128 + (high if base else low)


def condense_blocks(coef_ref, coupling_ref, pay_a, pay_b):
    sub = iota((8, LANES), 0)
    for j in range(EFACES):

        def body(k, sums):
            coef = coef_ref[pl.ds(k, 1), :]
            c = coupling_ref[k, j * FNODES : (j + 1) * FNODES, :].astype(F32)
            c0, c1 = c[0:8], c[8:16]
            u0, u1 = c0 * coef, c1 * coef
            new = []
            for d in range(5):
                new.append(sums[len(new)] + u0 * (pltpu.roll(c0, 8 - d, 0) if d else c0))
            for d in range(5):
                new.append(sums[len(new)] + u1 * (pltpu.roll(c1, 8 - d, 0) if d else c1))
            for d in range(8):
                new.append(sums[len(new)] + u0 * (pltpu.roll(c1, 8 - d, 0) if d else c1))
            return tuple(new)

        zero = jnp.zeros((8, LANES), F32)
        start = [zero] * 18
        start[0] = start[5] = zero + TAU_STAB
        sums = lax.fori_loop(0, MODES, body, tuple(start), unroll=8)
        at = pl.ds(j * LANES, LANES)
        for d in range(4):
            pay_a[pl.ds(d * 8, 8), at] = sums[d]
            pay_a[pl.ds(32 + d * 8, 8), at] = sums[5 + d]
        for d in range(8):
            pay_a[pl.ds(64 + d * 8, 8), at] = sums[10 + d]
        pay_b[pl.ds(0, 8), at] = jnp.where(sub < 4, sums[4], sums[9])


def condense_loads(weighted_ref, coupling_ref, face_ref, pay_b):
    for j in range(EFACES):

        def body(k, sums):
            c = coupling_ref[k, j * FNODES : (j + 1) * FNODES, :].astype(F32)
            return tuple(
                sums[comp] + c * weighted_ref[comp, pl.ds(k, 1), :] for comp in range(COMPS)
            )

        start = (jnp.zeros((FNODES, LANES), F32),) * COMPS
        sums = lax.fori_loop(0, MODES, body, start, unroll=8)
        at = pl.ds(j * LANES, LANES)
        for comp in range(COMPS):
            pay_b[pl.ds(8 + comp * FNODES, FNODES), at] = (
                face_ref[comp, j * FNODES : (j + 1) * FNODES, :] - sums[comp]
            )
        pay_b[pl.ds(88, LANES - 88), at] = jnp.zeros((LANES - 88, LANES), F32)


def pick(hot, parts):
    found = dot(hot, parts, NT)
    return found[:, 0:LANES] + found[:, LANES : 2 * LANES] + found[:, 2 * LANES :]


def pack_rest(rows, z, out_ref, q):
    lane = iota((8, LANES), 1)
    sub = iota((8, LANES), 0)
    rest = rows[pl.ds(z, CAP, stride=16), :]
    x0, x1, x2 = rest[0:8], rest[8:16], rest[16:24]
    out_ref[q, 0:8, :] = jnp.where(lane < 64, x0, pltpu.roll(x1, 64, 1))
    out_ref[q, 8:16, :] = jnp.where(
        lane < 64,
        x2,
        jnp.where(
            lane < 88, x0, jnp.where(lane < 112, pltpu.roll(x1, 24, 1), pltpu.roll(x2, 48, 1))
        ),
    )
    spread = pltpu.roll(x2, 48, 1, stride=8, stride_axis=0)
    out_ref[q, 16:17, :] = jnp.sum(
        jnp.where((lane >> 3) == sub, spread, 0.0), axis=0, keepdims=True
    )


def unpack_rest(arrived_ref, p, rows, z):
    lane = iota((8, LANES), 1)
    sub = iota((8, LANES), 0)
    b = arrived_ref[p, 0:8, :]
    c = arrived_ref[p, 8:16, :]
    tail = jnp.broadcast_to(arrived_ref[p, 16:17, :], (8, LANES))
    spread = jnp.take_along_axis(pltpu.roll(tail, 24, 1, stride=8, stride_axis=0), 7 - sub, axis=0)
    zero = jnp.zeros((8, LANES), F32)
    base = pl.multiple_of(z * CAP, 8)
    rows[pl.ds(base, 8), :] = jnp.where(lane < 64, b, jnp.where(lane < 88, c, zero))
    rows[pl.ds(base + 8, 8), :] = jnp.where(
        lane < 64, pltpu.roll(b, 64, 1), jnp.where(lane < 88, pltpu.roll(c, 104, 1), zero)
    )
    rows[pl.ds(base + 16, 8), :] = jnp.where(
        lane < 64,
        c,
        jnp.where(lane < 80, pltpu.roll(c, 80, 1), jnp.where(lane < 88, spread, zero)),
    )


def pack_traces(rows, z, ret_ref, p):
    lane = iota((8, LANES), 1)
    base = pl.multiple_of(z * CAP, 8)
    y0 = rows[pl.ds(base, 8), :]
    y1 = rows[pl.ds(base + 8, 8), :]
    y2 = rows[pl.ds(base + 16, 8), :]
    ret_ref[p, 0:8, :] = jnp.where(lane < 64, y0, pltpu.roll(y1, 64, 1))
    second = jnp.where(
        lane < 64,
        y2,
        jnp.where(lane < 80, y0, jnp.where(lane < 96, pltpu.roll(y1, 16, 1), pltpu.roll(y2, 32, 1))),
    )
    last = jnp.broadcast_to(pltpu.roll(second, 16, 1)[7:8], (8, LANES))
    last = pltpu.roll(last, 0, 1, stride=16, stride_axis=0)
    ret_ref[p, 8:15, :] = jnp.where(lane < 112, second, last)[0:7]


def unpack_traces(back_ref, q, rows, z):
    lane = iota((8, LANES), 1)
    sub = iota((8, LANES), 0)
    zero = jnp.zeros((8, LANES), F32)
    b = back_ref[q, 0:8, :]
    c = jnp.concatenate([back_ref[q, 8:15, :], zero[0:1]], axis=0)
    last = pltpu.roll(jnp.take_along_axis(c, 7 - sub, axis=0), 0, 1, stride=16, stride_axis=0)
    last = jnp.sum(jnp.where((lane >> 4) == sub - 1, last, 0.0), axis=0, keepdims=True)
    c = jnp.where(sub < 7, c, jnp.broadcast_to(last, (8, LANES)))
    y0 = jnp.where(lane < 64, b, jnp.where(lane < 80, c, zero))
    y1 = jnp.where(
        lane < 64, pltpu.roll(b, 64, 1), jnp.where(lane < 80, pltpu.roll(c, 112, 1), zero)
    )
    y2 = jnp.where(lane < 64, c, jnp.where(lane < 80, pltpu.roll(c, 96, 1), zero))
    rows[pl.ds(z, CAP, stride=16), :] = jnp.concatenate([y0, y1, y2], axis=0)


def solve_faces(grid, idle):
    scaled = []
    lower = []
    inverse = []
    for j in range(FNODES):
        column = jnp.stack([grid[block_row(i, j)] for i in range(j, FNODES)], axis=0)
        for k in range(j):
            column = column - scaled[k][j - k :] * lower[k][j - k][None]
        pivot = 1.0 / (column[0] + idle)
        inverse.append(pivot)
        scaled.append(column)
        lower.append(column * pivot[None])
    forward = []
    for i in range(FNODES):
        total = jnp.stack([grid[TRI + comp * FNODES + i] for comp in range(COMPS)], axis=0)
        for k in range(i):
            total = total - lower[k][i - k][None] * forward[k]
        forward.append(total)
    solved = [None] * FNODES
    for i in reversed(range(FNODES)):
        total = forward[i] * inverse[i][None]
        for k in range(i + 1, FNODES):
            total = total - lower[i][k - i][None] * solved[k]
        solved[i] = total
    return solved


def ring_offset(n):
    t = N_Z - 1 - n
    half = lax.div(t + 1, 2)
    return lax.rem(16 + half * (2 * lax.rem(t, 2) - 1), 16)


def spread_slots(lists, slots):
    lane = iota((4, LANES), 1)
    rows = [lists[pl.ds(a, 4, stride=3), :] for a in range(3)]
    for z in range(N_Z):
        a, b = divmod(z * CAP, LANES)
        value = pltpu.roll(rows[a], LANES - b, 1) if b else rows[a]
        if b + CAP > LANES:
            value = jnp.where(lane < LANES - b, value, pltpu.roll(rows[a + 1], LANES - b, 1))
        slots[pl.ds(z, 4, stride=N_Z), :] = jnp.where(lane < CAP, value, SLOTS)


def step_kernel(
    density_hbm,
    speed_hbm,
    flags_hbm,
    mass_hbm,
    eigs_hbm,
    send_hbm,
    face_hbm,
    coupling_hbm,
    inner_hbm,
    faceres_hbm,
    traces_ref,
    coef_ref,
    density,
    speed_ref,
    flags,
    mass,
    eigs_ref,
    lists,
    face_ref,
    coupling,
    inner,
    faceres,
    slots_ref,
    weighted,
    eps_out,
    eps_in,
    visc_out,
    visc_in,
    top_out,
    tops,
    slot_hot,
    row_hot,
    pay_a,
    pay_b,
    parts_a,
    parts_b,
    rows,
    whole_out,
    whole_in,
    rest_out,
    rest_in,
    joined_a,
    joined_b,
    grid,
    answer,
    returning,
    back,
    load_sem,
    send_a,
    recv_a,
    send_b,
    recv_b,
    send_c,
    recv_c,
    send_d,
    recv_d,
    send_e,
    recv_e,
    send_f,
    recv_f,
):
    me = lax.axis_index("dom")
    group = lax.axis_index("group")
    my_y = lax.div(me, N_Z)
    my_z = lax.rem(me, N_Z)
    following = {"dom": lax.rem(me + 1, N_DOM)}
    barrier = pltpu.get_barrier_semaphore()

    def each_peer(act):
        def one_z(n, carry):
            z = lax.rem(my_z + ring_offset(n), N_Z)
            for dy in (2, 1, 3, 0):
                act(lax.rem(my_y + dy, N_Y) * N_Z + z)
            return carry

        lax.fori_loop(0, N_Z - 1, one_z, 0)
        for dy in (2, 1, 3):
            act(lax.rem(my_y + dy, N_Y) * N_Z + my_z)

    def each_group(act):
        def one(k, carry):
            act(lax.rem(group + k, N_GROUP))
            return carry

        lax.fori_loop(1, N_GROUP, one, 0)

    each_peer(
        lambda q: pl.semaphore_signal(barrier, inc=1, device_id={"dom": q}, device_id_type=MESH)
    )
    each_group(
        lambda g: pl.semaphore_signal(barrier, inc=1, device_id={"group": g}, device_id_type=MESH)
    )
    loads = [
        pltpu.make_async_copy(source, target, load_sem.at[n])
        for n, (source, target) in enumerate(
            (
                (density_hbm, density),
                (speed_hbm, speed_ref),
                (flags_hbm, flags),
                (send_hbm, lists),
                (face_hbm, face_ref),
                (mass_hbm, mass),
                (eigs_hbm, eigs_ref),
                (coupling_hbm, coupling),
                (inner_hbm, inner),
                (faceres_hbm, faceres),
            )
        )
    ]
    for copy in loads:
        copy.start()
    for copy in loads[:5]:
        copy.wait()

    speed = speed_ref[...]
    eps = element_eps(density[...], speed, flags[...])
    spread_slots(lists, slots_ref)
    slots = slots_ref[...]
    lane = iota((N_DOM, LANES), 1)
    values = jnp.take_along_axis(
        jnp.broadcast_to(eps, (N_DOM, LANES)), slots & (ELEM_DEV - 1), axis=1
    )
    values = jnp.where(slots < SLOTS, values, 0.0)
    values = jnp.where(lane == LANES - 1, jnp.max(speed, axis=1, keepdims=True), values)
    for q in range(N_DOM):
        eps_out[q] = values[q : q + 1, :]

    for y in range(N_Y):
        for i in range(CAP):
            column = slots[y * N_Z : (y + 1) * N_Z, i : i + 1]
            slot_hot[y, i * N_Z : (i + 1) * N_Z, :] = one_hot(iota((N_Z, SLOTS), 1) == column)

    pl.semaphore_wait(barrier, N_DOM + N_GROUP - 2)
    each_peer(
        lambda q: remote(eps_out.at[q], eps_in.at[me], send_a, recv_a, {"dom": q}).start()
    )
    eps_in[me] = eps_out[me]
    partner_p, partner_i = partner_rows(face_ref)
    others = pl.ds(0, N_DOM - 1)
    whole = remote(eps_out.at[others], eps_in.at[others], send_a, recv_a, following)
    whole.wait_recv()
    whole.wait_send()

    partner_eps = jnp.zeros((16, LANES), F32)
    top = jnp.zeros((1, LANES), F32)
    for p in range(N_DOM):
        row = eps_in[p]
        top = jnp.maximum(top, row)
        found = jnp.take_along_axis(jnp.broadcast_to(row, (16, LANES)), partner_i, axis=1)
        partner_eps = jnp.where(partner_p == p, found, partner_eps)
    for r in range(16):
        visc_out[r] = partner_eps[r : r + 1, :]
    top_out[0] = top
    each_peer(
        lambda p: remote(
            visc_out.at[lax.div(p, 4)], visc_in.at[me], send_b, recv_b, {"dom": p}
        ).start()
    )
    each_group(
        lambda g: remote(top_out.at[0], tops.at[group], send_c, recv_c, {"group": g}).start()
    )
    visc_in[me] = visc_out[lax.div(me, 4)]
    tops[group] = top_out[0]

    for y in range(N_Y):
        received = iota((PART, FACES), 0) + y * PART
        row_hot[y] = one_hot(
            jnp.logical_or(received == face_ref[0:1, :], received == face_ref[1:2, :])
        )
    for copy in loads[5:]:
        copy.wait()

    whole = remote(eps_in.at[others], visc_in.at[others], send_b, recv_b, following)
    whole.wait_recv()
    whole.wait_send()
    seven = pl.ds(0, N_GROUP - 1)
    whole = remote(
        tops.at[seven],
        tops.at[seven],
        send_c,
        recv_c,
        {"group": lax.rem(group + 1, N_GROUP)},
    )
    whole.wait_recv()
    whole.wait_send()

    came = jnp.concatenate([visc_in[q] for q in range(N_DOM)], axis=0)
    came = pltpu.roll(came, lax.rem(4 - lax.rem(me, 4), 4) * 32, 1)
    total = jnp.zeros((N_DOM, LANES), F32)
    for i in range(CAP):
        slot = slots[:, i : i + 1]
        here = jnp.logical_and((slot & (ELEM_DEV - 1)) == lane, slot < SLOTS)
        total = total + jnp.where(here, came[:, i : i + 1], 0.0)
    gathered = jnp.sum(total, axis=0, keepdims=True)
    nu = NU_BASE + (EFACES * eps + gathered) / (2.0 * EFACES)
    top = tops[0]
    for g in range(1, N_GROUP):
        top = jnp.maximum(top, tops[g])
    peak = jnp.max(jnp.where(iota((1, LANES), 1) == LANES - 1, top, 0.0), axis=1, keepdims=True)
    square = iota((MODES, MODES), 0) == iota((MODES, MODES), 1)
    eigs = jnp.sum(jnp.where(square, eigs_ref[...], 0.0), axis=1, keepdims=True)
    coef = 1.0 / (mass[...] * (1.0 + speed / peak + nu * eigs))
    coef_ref[...] = coef

    condense_blocks(coef_ref, coupling, pay_a, pay_b)
    parts_a[...] = jnp.concatenate(split3(pay_a[...]), axis=0)
    for c in range(N_Y):
        y = lax.rem(my_y + c, N_Y)
        rows[...] = pick(slot_hot[y], parts_a[...])

        def send_whole(n, carry):
            z = lax.rem(my_z + ring_offset(n), N_Z)
            q = y * N_Z + z
            whole_out[q] = rows[pl.ds(z, CAP, stride=16), :]
            remote(whole_out.at[q], whole_in.at[me], send_d, recv_d.at[c], {"dom": q}).start()
            return carry

        lax.fori_loop(0, N_Z if c else N_Z - 1, send_whole, 0)
        if c == 0:
            whole_in[me] = rows[pl.ds(my_z, CAP, stride=16), :]
    weighted[...] = inner[...] * coef[None]
    condense_loads(weighted, coupling, faceres, pay_b)
    parts_b[...] = jnp.concatenate(split3(pay_b[...]), axis=0)
    for c in range(N_Y):
        y = lax.rem(my_y + c, N_Y)
        rows[...] = pick(slot_hot[y], parts_b[...])

        def send_rest(n, carry):
            z = lax.rem(my_z + ring_offset(n), N_Z)
            q = y * N_Z + z
            pack_rest(rows, z, rest_out, q)
            remote(rest_out.at[q], rest_in.at[me], send_e, recv_e.at[c], {"dom": q}).start()
            return carry

        lax.fori_loop(0, N_Z if c else N_Z - 1, send_rest, 0)
        if c == 0:
            pack_rest(rows, my_z, rest_in, me)

    def to_grid(joined, start, height):
        for chunk in range(6):
            for n in range(height // 8):
                grid[start + n * 8 : start + n * 8 + 8, chunk, :] = joined[
                    n * 8 : n * 8 + 8, chunk * LANES : (chunk + 1) * LANES
                ]

    for c in range(N_Y):
        y = lax.rem(my_y + N_Y - c, N_Y)
        sources = pl.ds(0, N_Z if c else N_Z - 1)
        remote(
            whole_out.at[sources], whole_in.at[sources], send_d, recv_d.at[c], following
        ).wait_recv()
        came = whole_in[pl.ds(pl.multiple_of(y * N_Z, N_Z), N_Z)].reshape(PART, LANES)
        stacked = jnp.concatenate(split3(jnp.transpose(came)), axis=0)
        found = dot(stacked, row_hot[y], NN)
        found = found[0:LANES] + found[LANES : 2 * LANES] + found[2 * LANES :]
        joined_a[...] = found if c == 0 else joined_a[...] + found
    to_grid(joined_a, 0, LANES)
    remote(whole_out.at[others], whole_in.at[others], send_d, recv_d.at[0], following).wait_send()
    for c in range(N_Y):
        y = lax.rem(my_y + N_Y - c, N_Y)
        sources = pl.ds(0, N_Z if c else N_Z - 1)
        remote(
            rest_out.at[sources], rest_in.at[sources], send_e, recv_e.at[c], following
        ).wait_recv()

        def take_rest(z, carry):
            unpack_rest(rest_in, y * N_Z + z, rows, z)
            return carry

        lax.fori_loop(0, N_Z, take_rest, 0, unroll=2)
        stacked = jnp.concatenate(split3(jnp.transpose(rows[...])[0:HALF]), axis=0)
        found = dot(stacked, row_hot[y], NN)
        found = found[0:HALF] + found[HALF : 2 * HALF] + found[2 * HALF :]
        joined_b[...] = found if c == 0 else joined_b[...] + found
    to_grid(joined_b, LANES, USED - LANES)
    first = face_ref[0:1, :]
    idle = jnp.concatenate(
        [first[:, chunk * LANES : (chunk + 1) * LANES] for chunk in range(6)]
        + [jnp.full((2, LANES), ROWS, I32)],
        axis=0,
    )
    idle = jnp.where(idle < ROWS, 0.0, 1.0)
    solved = solve_faces(grid, idle)
    for i in range(FNODES):
        for comp in range(COMPS):
            answer[comp * FNODES + i] = solved[i][comp]
    face_traces = jnp.concatenate([answer[:, chunk, :] for chunk in range(6)], axis=1)
    gap = jnp.zeros((LANES - COMPS * FNODES, FACES), BF16)
    high, low = split2(face_traces)
    both = jnp.concatenate([high, gap, low, gap], axis=0)

    for c in range(N_Y):
        y = lax.rem(my_y + c, N_Y)
        found = dot(row_hot[y], both, NT)
        rows[...] = found[:, 0:LANES] + found[:, LANES : 2 * LANES]

        def send_traces(n, carry):
            z = lax.rem(my_z + ring_offset(n), N_Z)
            p = y * N_Z + z
            pack_traces(rows, z, returning, p)
            remote(returning.at[p], back.at[me], send_f, recv_f.at[c], {"dom": p}).start()
            return carry

        lax.fori_loop(0, N_Z if c else N_Z - 1, send_traces, 0)
        if c == 0:
            pack_traces(rows, my_z, back, me)

    for c in range(N_Y):
        y = lax.rem(my_y + N_Y - c, N_Y)
        sources = pl.ds(0, N_Z if c else N_Z - 1)
        remote(returning.at[sources], back.at[sources], send_f, recv_f.at[c], following).wait_recv()

        def take_traces(z, carry):
            unpack_traces(back, y * N_Z + z, rows, z)
            return carry

        lax.fori_loop(0, N_Z, take_traces, 0, unroll=2)
        turned = jnp.transpose(rows[...])[0 : COMPS * FNODES]
        stacked = jnp.concatenate(split2(turned), axis=0)
        found = dot(stacked, slot_hot[y], NN)
        found = found[0 : COMPS * FNODES] + found[COMPS * FNODES :]
        for comp in range(COMPS):
            for j in range(EFACES):
                piece = found[comp * FNODES : (comp + 1) * FNODES, j * LANES : (j + 1) * LANES]
                at = slice(j * FNODES, (j + 1) * FNODES)
                traces_ref[comp, at, :] = piece if c == 0 else traces_ref[comp, at, :] + piece
    remote(rest_out.at[others], rest_in.at[others], send_e, recv_e.at[0], following).wait_send()
    remote(returning.at[others], back.at[others], send_f, recv_f.at[0], following).wait_send()


def update_kernel(traces_in, coef_ref, coupling_ref, inner_ref, update_ref, traces_ref):
    traces_ref[...] = traces_in[...]

    def substitute(k, carry):
        c = coupling_ref[k].astype(F32)
        coef = coef_ref[pl.ds(k, 1), :]
        for comp in range(COMPS):
            pulled = jnp.sum(c * traces_in[comp], axis=0, keepdims=True)
            update_ref[comp, pl.ds(k, 1), :] = coef * (inner_ref[comp, pl.ds(k, 1), :] - pulled)
        return carry

    lax.fori_loop(0, MODES, substitute, 0, unroll=4)


def local(
    density_modes,
    wave_speed,
    shock_flags,
    elem_mass,
    stiff_eigs,
    coupling,
    interior_res,
    face_res,
    send_rows,
    face_rows,
):
    vmem = pl.BlockSpec(memory_space=pltpu.VMEM)
    anywhere = pl.BlockSpec(memory_space=pltpu.HBM)
    dma = pltpu.SemaphoreType.DMA
    traces, coef = pl.pallas_call(
        step_kernel,
        out_shape=(
            jax.ShapeDtypeStruct((COMPS, TRACE, LANES), F32),
            jax.ShapeDtypeStruct((MODES, LANES), F32),
        ),
        in_specs=[anywhere] * 10,
        out_specs=(vmem, vmem),
        scratch_shapes=[
            pltpu.VMEM((MODES, LANES), F32),
            pltpu.VMEM((1, LANES), F32),
            pltpu.VMEM((1, LANES), I32),
            pltpu.VMEM((1, LANES), F32),
            pltpu.VMEM((1, MODES), F32),
            pltpu.VMEM((12, LANES), I32),
            pltpu.VMEM((2, FACES), I32),
            pltpu.VMEM((MODES, TRACE, LANES), BF16),
            pltpu.VMEM((COMPS, MODES, LANES), F32),
            pltpu.VMEM((COMPS, TRACE, LANES), F32),
            pltpu.VMEM((N_DOM, LANES), I32),
            pltpu.VMEM((COMPS, MODES, LANES), F32),
            pltpu.VMEM((N_DOM, 1, LANES), F32),
            pltpu.VMEM((N_DOM, 1, LANES), F32),
            pltpu.VMEM((16, 1, LANES), F32),
            pltpu.VMEM((N_DOM, 1, LANES), F32),
            pltpu.VMEM((1, 1, LANES), F32),
            pltpu.VMEM((N_GROUP, 1, LANES), F32),
            pltpu.VMEM((N_Y, PART, SLOTS), BF16),
            pltpu.VMEM((N_Y, PART, FACES), BF16),
            pltpu.VMEM((LANES, SLOTS), F32),
            pltpu.VMEM((LANES, SLOTS), F32),
            pltpu.VMEM((3 * LANES, SLOTS), BF16),
            pltpu.VMEM((3 * LANES, SLOTS), BF16),
            pltpu.VMEM((PART, LANES), F32),
            pltpu.VMEM((N_DOM, CAP, LANES), F32),
            pltpu.VMEM((N_DOM, CAP, LANES), F32),
            pltpu.VMEM((N_DOM, REST_TILE, LANES), F32),
            pltpu.VMEM((N_DOM, REST_TILE, LANES), F32),
            pltpu.VMEM((LANES, FACES), F32),
            pltpu.VMEM((HALF, FACES), F32),
            pltpu.VMEM((USED, 8, LANES), F32),
            pltpu.VMEM((COMPS * FNODES, 8, LANES), F32),
            pltpu.VMEM((N_DOM, RET_TILE, LANES), F32),
            pltpu.VMEM((N_DOM, RET_TILE, LANES), F32),
            dma((10,)),
            dma,
            dma,
            dma,
            dma,
            dma,
            dma,
            dma,
            dma((N_Y,)),
            dma,
            dma((N_Y,)),
            dma,
            dma((N_Y,)),
        ],
        compiler_params=pltpu.CompilerParams(
            collective_id=0, has_side_effects=True, vmem_limit_bytes=VMEM_LIMIT
        ),
        name="newton_step",
    )(
        density_modes,
        wave_speed[None, :],
        shock_flags[None, :],
        elem_mass[None, :],
        stiff_eigs[None, :],
        send_rows.reshape(12, LANES),
        face_rows,
        coupling,
        interior_res,
        face_res,
    )
    return pl.pallas_call(
        update_kernel,
        out_shape=(
            jax.ShapeDtypeStruct((COMPS, MODES, LANES), F32),
            jax.ShapeDtypeStruct((COMPS, TRACE, LANES), F32),
        ),
        in_specs=[vmem] * 4,
        out_specs=(vmem, vmem),
        compiler_params=pltpu.CompilerParams(vmem_limit_bytes=16 * 1024 * 1024),
        name="back_substitute",
    )(traces, coef, coupling, interior_res)


def solution(mesh):
    return jax.shard_map(
        local,
        mesh=mesh,
        in_specs=(
            P(None, ("group", "dom")),
            P(("group", "dom")),
            P(("group", "dom")),
            P(("group", "dom")),
            P(),
            P(None, None, ("group", "dom")),
            P(None, None, ("group", "dom")),
            P(None, None, ("group", "dom")),
            P(("group", "dom")),
            P(None, ("group", "dom")),
        ),
        out_specs=(P(None, None, ("group", "dom")), P(None, None, ("group", "dom"))),
        check_vma=False,
    )
```

time: 140 us -> 131 us (0.936)
  Pallas kernels: 133 us -> 127 us
  local copies, waits for them, and re-layouts: 4.64 us -> 1.7 us
    pallas_call x1 -> x2, Pallas kernels: 133 us -> 127 us  [the longest x1 125 us: local(): pl.pallas_call(step_kernel, out_shape=(jax.ShapeDtypeStruct((COMPS, TRACE...]
    unnamed x2 -> x8, local copies, waits for them, and re-layouts: 3.25 us -> 1.7 us
where the time goes in v3:
time: 131 us; the launch traced here: 130 us
  Pallas kernels  127 us (97%)
  local copies, waits for them, and re-layouts  1.7 us (1%)
    pallas_call x1, Pallas kernels, local(): pl.pallas_call(step_kernel, out_shape=(jax.ShapeDtypeStruct((COMPS, TRACE...  125 us

profile of v3, /device:TPU:24, one launch (start us, length us, event | category | flops | bytes accessed | tf_op | source)
XLA Modules:
  0.0 129.6 jit_solution(15906423983610789747)
XLA Ops:
  0.6 0.0 copy-start.1
  0.6 0.0 copy-start
  0.7 124.7 %newton_step.1 = (f32[5,96,128]{2,1,0:T(8,128)}, f32[64,128]{1,0:T(8,128)}) custom-call(f32[64,128]{1,0:T(8,128)} %density_hbm.1, f32[1,128]{1,0:T(1,128)} %bitcast.6, s32[1,128]{1,0:T(1,128)} %bitcast.7, f32[1,128]{1,0:T(1,128)} %bitcast.8, f32[1,64]{1,0:T(1,128)} %bitcast.9, s32[12,128]{1,0:T(8,128)} %bitcast.5, s32[2,768]{1,0:T(2,128)} %face_hbm.1, ...), custom_call_target="tpu_custom_call" | custom-call | tf_op jit(solution)/shard_map/newton_step/pallas_call | solution.py:678
  125.4 0.0 copy-done.1
  125.4 0.0 copy-done
  125.4 0.0 copy-start.2
  125.4 0.9 copy-done.2
  126.4 0.0 copy-start.3
  126.4 0.8 copy-done.3
  127.1 2.4 %back_substitute.1 = (f32[5,64,128]{2,1,0:T(8,128)}, f32[5,96,128]{2,1,0:T(8,128)}) custom-call(f32[5,96,128]{2,1,0:T(8,128)S(1)} %copy-done.2, f32[64,128]{1,0:T(8,128)S(1)} %copy-done.3, bf16[64,96,128]{2,1,0:T(8,128)(2,1)S(1)} %copy-done, f32[5,64,128]{2,1,0:T(8,128)S(1)} %copy-done.1), custom_call_target="tpu_custom_call" | custom-call | tf_op jit(solution)/shard_map/back_substitute/pallas_call | solution.py:752
Async XLA Ops:
  0.6 124.8 %copy-start.1 = (f32[5,64,128]{2,1,0:T(8,128)S(1)}, f32[5,64,128]{2,1,0:T(8,128)}, u32[]{:S(2)}) copy-start(f32[5,64,128]{2,1,0:T(8,128)} %inner_ref.1) | copy-start | bytes 491524
  0.6 124.8 %copy-start = (bf16[64,96,128]{2,1,0:T(8,128)(2,1)S(1)}, bf16[64,96,128]{2,1,0:T(8,128)(2,1)}, u32[]{:S(2)}) copy-start(bf16[64,96,128]{2,1,0:T(8,128)(2,1)} %coupling_ref.1) | copy-start | bytes 4718596
  125.4 0.9 copy-start.2
  126.4 0.8 copy-start.3

commit v4 on v3

--- a/solution.py
+++ b/solution.py
@@ -23,9 +23,12 @@
 N_Y = N_DOM // N_Z
 PART = N_Z * CAP
 LANES = 128
-HALF = 96
-REST_TILE = 17
-RET_TILE = 15
+HALF = 48
+EARLY = 2
+FIRST_TILE = 8
+LOAD_TILE = 9
+EARLY_TILE = 6
+LATE_TILE = 9
 
 EPS_SCALE = 0.1
 NU_BASE = 0.02
@@ -143,35 +146,40 @@
     return 128 + (high if base else low)
 
 
-def condense_blocks(coef_ref, coupling_ref, pay_a, pay_b):
+def multiply_blocks(coupling_ref, products):
     sub = iota((8, LANES), 0)
-    for j in range(EFACES):
-
-        def body(k, sums):
-            coef = coef_ref[pl.ds(k, 1), :]
+
+    def body(k, carry):
+        for j in range(EFACES):
             c = coupling_ref[k, j * FNODES : (j + 1) * FNODES, :].astype(F32)
             c0, c1 = c[0:8], c[8:16]
-            u0, u1 = c0 * coef, c1 * coef
-            new = []
-            for d in range(5):
-                new.append(sums[len(new)] + u0 * (pltpu.roll(c0, 8 - d, 0) if d else c0))
-            for d in range(5):
-                new.append(sums[len(new)] + u1 * (pltpu.roll(c1, 8 - d, 0) if d else c1))
+            turned = [c1] + [pltpu.roll(c1, 8 - d, 0) for d in range(1, 8)]
+            for d in range(4):
+                products[j, k, d * 8 : d * 8 + 8, :] = c0 * (pltpu.roll(c0, 8 - d, 0) if d else c0)
+                products[j, k, 32 + d * 8 : 40 + d * 8, :] = c1 * turned[d]
             for d in range(8):
-                new.append(sums[len(new)] + u0 * (pltpu.roll(c1, 8 - d, 0) if d else c1))
-            return tuple(new)
-
-        zero = jnp.zeros((8, LANES), F32)
-        start = [zero] * 18
-        start[0] = start[5] = zero + TAU_STAB
-        sums = lax.fori_loop(0, MODES, body, tuple(start), unroll=8)
+                products[j, k, 64 + d * 8 : 72 + d * 8, :] = c0 * turned[d]
+            products[j, k, 128:136, :] = jnp.where(
+                sub < 4, c0 * pltpu.roll(c0, 4, 0), c1 * turned[4]
+            )
+        return carry
+
+    lax.fori_loop(0, MODES, body, 0)
+
+
+def condense_blocks(coef_ref, products, parts_a, pay_b):
+    for j in range(EFACES):
+
+        def body(k, sums):
+            return sums + coef_ref[pl.ds(k, 1), :] * products[j, k]
+
+        row = iota((TRI, LANES), 0)
+        diagonal = jnp.logical_or(row < 8, jnp.logical_and(row >= 32, row < 40))
+        start = jnp.where(diagonal, TAU_STAB, 0.0)
+        sums = lax.fori_loop(0, MODES, body, start, unroll=8)
         at = pl.ds(j * LANES, LANES)
-        for d in range(4):
-            pay_a[pl.ds(d * 8, 8), at] = sums[d]
-            pay_a[pl.ds(32 + d * 8, 8), at] = sums[5 + d]
-        for d in range(8):
-            pay_a[pl.ds(64 + d * 8, 8), at] = sums[10 + d]
-        pay_b[pl.ds(0, 8), at] = jnp.where(sub < 4, sums[4], sums[9])
+        parts_a[:, at] = jnp.concatenate(split3(sums[0:LANES]), axis=0)
+        pay_b[pl.ds(0, 8), at] = sums[LANES:TRI]
 
 
 def condense_loads(weighted_ref, coupling_ref, face_ref, pay_b):
@@ -198,104 +206,116 @@
     return found[:, 0:LANES] + found[:, LANES : 2 * LANES] + found[:, 2 * LANES :]
 
 
-def pack_rest(rows, z, out_ref, q):
+def pack_first(x0, x1, x2, out_ref, q):
+    lane = iota((8, LANES), 1)
+    out_ref[q] = jnp.where(
+        lane < 40, x0, jnp.where(lane < 80, pltpu.roll(x1, 40, 1), pltpu.roll(x2, 80, 1))
+    )
+
+
+def unpack_first(tile):
+    lane = iota((8, LANES), 1)
+    zero = jnp.zeros((8, LANES), F32)
+    return [
+        jnp.where(lane < 40, x, zero) for x in (tile, pltpu.roll(tile, 88, 1), pltpu.roll(tile, 48, 1))
+    ]
+
+
+def pack48(x0, x1, x2, out_ref, q):
     lane = iota((8, LANES), 1)
     sub = iota((8, LANES), 0)
-    rest = rows[pl.ds(z, CAP, stride=16), :]
-    x0, x1, x2 = rest[0:8], rest[8:16], rest[16:24]
-    out_ref[q, 0:8, :] = jnp.where(lane < 64, x0, pltpu.roll(x1, 64, 1))
-    out_ref[q, 8:16, :] = jnp.where(
-        lane < 64,
-        x2,
-        jnp.where(
-            lane < 88, x0, jnp.where(lane < 112, pltpu.roll(x1, 24, 1), pltpu.roll(x2, 48, 1))
-        ),
-    )
-    spread = pltpu.roll(x2, 48, 1, stride=8, stride_axis=0)
-    out_ref[q, 16:17, :] = jnp.sum(
-        jnp.where((lane >> 3) == sub, spread, 0.0), axis=0, keepdims=True
-    )
-
-
-def unpack_rest(arrived_ref, p, rows, z):
-    lane = iota((8, LANES), 1)
-    sub = iota((8, LANES), 0)
-    b = arrived_ref[p, 0:8, :]
-    c = arrived_ref[p, 8:16, :]
-    tail = jnp.broadcast_to(arrived_ref[p, 16:17, :], (8, LANES))
-    spread = jnp.take_along_axis(pltpu.roll(tail, 24, 1, stride=8, stride_axis=0), 7 - sub, axis=0)
-    zero = jnp.zeros((8, LANES), F32)
-    base = pl.multiple_of(z * CAP, 8)
-    rows[pl.ds(base, 8), :] = jnp.where(lane < 64, b, jnp.where(lane < 88, c, zero))
-    rows[pl.ds(base + 8, 8), :] = jnp.where(
-        lane < 64, pltpu.roll(b, 64, 1), jnp.where(lane < 88, pltpu.roll(c, 104, 1), zero)
-    )
-    rows[pl.ds(base + 16, 8), :] = jnp.where(
-        lane < 64,
-        c,
-        jnp.where(lane < 80, pltpu.roll(c, 80, 1), jnp.where(lane < 88, spread, zero)),
-    )
-
-
-def pack_traces(rows, z, ret_ref, p):
-    lane = iota((8, LANES), 1)
-    base = pl.multiple_of(z * CAP, 8)
-    y0 = rows[pl.ds(base, 8), :]
-    y1 = rows[pl.ds(base + 8, 8), :]
-    y2 = rows[pl.ds(base + 16, 8), :]
-    ret_ref[p, 0:8, :] = jnp.where(lane < 64, y0, pltpu.roll(y1, 64, 1))
-    second = jnp.where(
-        lane < 64,
-        y2,
-        jnp.where(lane < 80, y0, jnp.where(lane < 96, pltpu.roll(y1, 16, 1), pltpu.roll(y2, 32, 1))),
-    )
-    last = jnp.broadcast_to(pltpu.roll(second, 16, 1)[7:8], (8, LANES))
-    last = pltpu.roll(last, 0, 1, stride=16, stride_axis=0)
-    ret_ref[p, 8:15, :] = jnp.where(lane < 112, second, last)[0:7]
-
-
-def unpack_traces(back_ref, q, rows, z):
+    turned = pltpu.roll(x2, 96, 1)
+    out_ref[q, 0:8, :] = jnp.where(
+        lane < 48, x0, jnp.where(lane < 96, pltpu.roll(x1, 48, 1), turned)
+    )
+    spread = pltpu.roll(turned, 0, 1, stride=16, stride_axis=0)
+    out_ref[q, 8:9, :] = jnp.sum(jnp.where((lane >> 4) == sub, spread, 0.0), axis=0, keepdims=True)
+
+
+def unpack48(tile, tail):
     lane = iota((8, LANES), 1)
     sub = iota((8, LANES), 0)
     zero = jnp.zeros((8, LANES), F32)
-    b = back_ref[q, 0:8, :]
-    c = jnp.concatenate([back_ref[q, 8:15, :], zero[0:1]], axis=0)
-    last = pltpu.roll(jnp.take_along_axis(c, 7 - sub, axis=0), 0, 1, stride=16, stride_axis=0)
-    last = jnp.sum(jnp.where((lane >> 4) == sub - 1, last, 0.0), axis=0, keepdims=True)
-    c = jnp.where(sub < 7, c, jnp.broadcast_to(last, (8, LANES)))
-    y0 = jnp.where(lane < 64, b, jnp.where(lane < 80, c, zero))
-    y1 = jnp.where(
-        lane < 64, pltpu.roll(b, 64, 1), jnp.where(lane < 80, pltpu.roll(c, 112, 1), zero)
-    )
-    y2 = jnp.where(lane < 64, c, jnp.where(lane < 80, pltpu.roll(c, 96, 1), zero))
-    rows[pl.ds(z, CAP, stride=16), :] = jnp.concatenate([y0, y1, y2], axis=0)
-
-
-def solve_faces(grid, idle):
+    spread = pltpu.roll(jnp.broadcast_to(tail, (8, LANES)), 48, 1)
+    spread = pltpu.roll(spread, 0, 1, stride=16, stride_axis=0)
+    spread = jnp.take_along_axis(spread, 7 - sub, axis=0)
+    return [
+        jnp.where(lane < 48, tile, zero),
+        jnp.where(lane < 48, pltpu.roll(tile, 80, 1), zero),
+        jnp.where(lane < 32, pltpu.roll(tile, 32, 1), jnp.where(lane < 48, spread, zero)),
+    ]
+
+
+def pack32(x0, x1, x2, out_ref, q):
+    lane = iota((8, LANES), 1)
+    sub = iota((8, LANES), 0)
+    full = jnp.where(
+        lane < 32, x0, jnp.where(lane < 64, pltpu.roll(x1, 32, 1), pltpu.roll(x2, 64, 1))
+    )
+    extra = jnp.zeros((8, LANES), F32)
+    for c in range(3):
+        turned = pltpu.roll(full, 96 - 32 * c, 1)
+        extra = jnp.where(sub == c, jnp.broadcast_to(turned[6:7], (8, LANES)), extra)
+        extra = jnp.where(sub == 3 + c, jnp.broadcast_to(turned[7:8], (8, LANES)), extra)
+    out_ref[q] = jnp.where(lane < 96, full, extra)[0:6]
+
+
+def unpack32(tile):
+    lane = iota((8, LANES), 1)
+    sub = iota((8, LANES), 0)
+    zero = jnp.zeros((8, LANES), F32)
+    full = jnp.concatenate([tile, zero[0:2]], axis=0)
+    turned = [pltpu.roll(full, 32 * c + 32, 1) for c in range(3)]
+    one = lane[0:1]
+    for r in range(2):
+        row = jnp.where(
+            one < 32,
+            turned[0][3 * r : 3 * r + 1],
+            jnp.where(one < 64, turned[1][3 * r + 1 : 3 * r + 2], turned[2][3 * r + 2 : 3 * r + 3]),
+        )
+        full = jnp.where(sub == 6 + r, jnp.broadcast_to(row, (8, LANES)), full)
+    return [
+        jnp.where(lane < 32, x, zero) for x in (full, pltpu.roll(full, 96, 1), pltpu.roll(full, 64, 1))
+    ]
+
+
+def thirds(x):
+    return x[0:8], x[8:16], x[16:24]
+
+
+def lower_row(i, k):
+    return k * FNODES - k * (k - 1) // 2 + i - k
+
+
+def factor_faces(grid, idle, lower_ref, inverse_ref):
     scaled = []
     lower = []
-    inverse = []
     for j in range(FNODES):
         column = jnp.stack([grid[block_row(i, j)] for i in range(j, FNODES)], axis=0)
         for k in range(j):
             column = column - scaled[k][j - k :] * lower[k][j - k][None]
         pivot = 1.0 / (column[0] + idle)
-        inverse.append(pivot)
+        inverse_ref[j] = pivot
         scaled.append(column)
         lower.append(column * pivot[None])
+        lower_ref[lower_row(j, j) : lower_row(j, j) + FNODES - j] = lower[j]
+
+
+def solve_faces(grid, lower_ref, inverse_ref, comps, answer):
     forward = []
     for i in range(FNODES):
-        total = jnp.stack([grid[TRI + comp * FNODES + i] for comp in range(COMPS)], axis=0)
+        total = jnp.stack([grid[TRI + comp * FNODES + i] for comp in comps], axis=0)
         for k in range(i):
-            total = total - lower[k][i - k][None] * forward[k]
+            total = total - lower_ref[lower_row(i, k)][None] * forward[k]
         forward.append(total)
     solved = [None] * FNODES
     for i in reversed(range(FNODES)):
-        total = forward[i] * inverse[i][None]
+        total = forward[i] * inverse_ref[i][None]
         for k in range(i + 1, FNODES):
-            total = total - lower[i][k - i][None] * solved[k]
+            total = total - lower_ref[lower_row(k, i)][None] * solved[k]
         solved[i] = total
-    return solved
+        for n, comp in enumerate(comps):
+            answer[comp * FNODES + i] = total[n]
 
 
 def ring_offset(n):
@@ -348,21 +368,28 @@
     tops,
     slot_hot,
     row_hot,
-    pay_a,
+    products,
+    masks,
     pay_b,
     parts_a,
     parts_b,
     rows,
     whole_out,
     whole_in,
-    rest_out,
-    rest_in,
+    first_out,
+    first_in,
+    loads_out,
+    loads_in,
     joined_a,
     joined_b,
     grid,
+    lower,
+    inverse,
     answer,
-    returning,
-    back,
+    early_out,
+    early_in,
+    late_out,
+    late_in,
     load_sem,
     send_a,
     recv_a,
@@ -376,6 +403,10 @@
     recv_e,
     send_f,
     recv_f,
+    send_g,
+    recv_g,
+    send_h,
+    recv_h,
 ):
     me = lax.axis_index("dom")
     group = lax.axis_index("group")
@@ -417,9 +448,9 @@
                 (flags_hbm, flags),
                 (send_hbm, lists),
                 (face_hbm, face_ref),
+                (coupling_hbm, coupling),
                 (mass_hbm, mass),
                 (eigs_hbm, eigs_ref),
-                (coupling_hbm, coupling),
                 (inner_hbm, inner),
                 (faceres_hbm, faceres),
             )
@@ -454,6 +485,8 @@
     )
     eps_in[me] = eps_out[me]
     partner_p, partner_i = partner_rows(face_ref)
+    loads[5].wait()
+    multiply_blocks(coupling, products)
     others = pl.ds(0, N_DOM - 1)
     whole = remote(eps_out.at[others], eps_in.at[others], send_a, recv_a, following)
     whole.wait_recv()
@@ -485,7 +518,11 @@
         row_hot[y] = one_hot(
             jnp.logical_or(received == face_ref[0:1, :], received == face_ref[1:2, :])
         )
-    for copy in loads[5:]:
+    for i in range(CAP):
+        slot = slots[:, i : i + 1]
+        here = jnp.logical_and((slot & (ELEM_DEV - 1)) == lane, slot < SLOTS)
+        masks[i] = jnp.where(here, 1.0, 0.0)
+    for copy in loads[6:]:
         copy.wait()
 
     whole = remote(eps_in.at[others], visc_in.at[others], send_b, recv_b, following)
@@ -506,9 +543,7 @@
     came = pltpu.roll(came, lax.rem(4 - lax.rem(me, 4), 4) * 32, 1)
     total = jnp.zeros((N_DOM, LANES), F32)
     for i in range(CAP):
-        slot = slots[:, i : i + 1]
-        here = jnp.logical_and((slot & (ELEM_DEV - 1)) == lane, slot < SLOTS)
-        total = total + jnp.where(here, came[:, i : i + 1], 0.0)
+        total = total + masks[i] * came[:, i : i + 1]
     gathered = jnp.sum(total, axis=0, keepdims=True)
     nu = NU_BASE + (EFACES * eps + gathered) / (2.0 * EFACES)
     top = tops[0]
@@ -520,8 +555,7 @@
     coef = 1.0 / (mass[...] * (1.0 + speed / peak + nu * eigs))
     coef_ref[...] = coef
 
-    condense_blocks(coef_ref, coupling, pay_a, pay_b)
-    parts_a[...] = jnp.concatenate(split3(pay_a[...]), axis=0)
+    condense_blocks(coef_ref, products, parts_a, pay_b)
     for c in range(N_Y):
         y = lax.rem(my_y + c, N_Y)
         rows[...] = pick(slot_hot[y], parts_a[...])
@@ -543,16 +577,30 @@
         y = lax.rem(my_y + c, N_Y)
         rows[...] = pick(slot_hot[y], parts_b[...])
 
+        def pack_rest(z, first_ref, loads_ref, q):
+            rest = rows[pl.ds(z, CAP, stride=16), :]
+            pack_first(*thirds(rest), first_ref, q)
+            pack48(*thirds(pltpu.roll(rest, 88, 1)), loads_ref, q)
+
         def send_rest(n, carry):
             z = lax.rem(my_z + ring_offset(n), N_Z)
             q = y * N_Z + z
-            pack_rest(rows, z, rest_out, q)
-            remote(rest_out.at[q], rest_in.at[me], send_e, recv_e.at[c], {"dom": q}).start()
+            pack_rest(z, first_out, loads_out, q)
+            remote(first_out.at[q], first_in.at[me], send_e, recv_e.at[c], {"dom": q}).start()
             return carry
 
         lax.fori_loop(0, N_Z if c else N_Z - 1, send_rest, 0)
         if c == 0:
-            pack_rest(rows, my_z, rest_in, me)
+            pack_rest(my_z, first_in, loads_in, me)
+    for c in range(N_Y):
+        y = lax.rem(my_y + c, N_Y)
+
+        def send_loads(n, carry):
+            q = y * N_Z + lax.rem(my_z + ring_offset(n), N_Z)
+            remote(loads_out.at[q], loads_in.at[me], send_g, recv_g.at[c], {"dom": q}).start()
+            return carry
+
+        lax.fori_loop(0, N_Z if c else N_Z - 1, send_loads, 0)
 
     def to_grid(joined, start, height):
         for chunk in range(6):
@@ -574,76 +622,109 @@
         joined_a[...] = found if c == 0 else joined_a[...] + found
     to_grid(joined_a, 0, LANES)
     remote(whole_out.at[others], whole_in.at[others], send_d, recv_d.at[0], following).wait_send()
-    for c in range(N_Y):
-        y = lax.rem(my_y + N_Y - c, N_Y)
-        sources = pl.ds(0, N_Z if c else N_Z - 1)
-        remote(
-            rest_out.at[sources], rest_in.at[sources], send_e, recv_e.at[c], following
-        ).wait_recv()
-
-        def take_rest(z, carry):
-            unpack_rest(rest_in, y * N_Z + z, rows, z)
-            return carry
-
-        lax.fori_loop(0, N_Z, take_rest, 0, unroll=2)
-        stacked = jnp.concatenate(split3(jnp.transpose(rows[...])[0:HALF]), axis=0)
-        found = dot(stacked, row_hot[y], NN)
-        found = found[0:HALF] + found[HALF : 2 * HALF] + found[2 * HALF :]
-        joined_b[...] = found if c == 0 else joined_b[...] + found
-    to_grid(joined_b, LANES, USED - LANES)
+
+    def take_rest(out_ref, in_ref, send_sem, recv_sem, unpack):
+        for c in range(N_Y):
+            y = lax.rem(my_y + N_Y - c, N_Y)
+            sources = pl.ds(0, N_Z if c else N_Z - 1)
+            remote(
+                out_ref.at[sources], in_ref.at[sources], send_sem, recv_sem.at[c], following
+            ).wait_recv()
+
+            def take(z, carry):
+                base = pl.multiple_of(z * CAP, 8)
+                rows[pl.ds(base, CAP), :] = jnp.concatenate(unpack(y * N_Z + z), axis=0)
+                return carry
+
+            lax.fori_loop(0, N_Z, take, 0, unroll=2)
+            stacked = jnp.concatenate(split3(jnp.transpose(rows[...])[0:HALF]), axis=0)
+            found = dot(stacked, row_hot[y], NN)
+            found = found[0:HALF] + found[HALF : 2 * HALF] + found[2 * HALF :]
+            joined_b[...] = found if c == 0 else joined_b[...] + found
+        remote(out_ref.at[others], in_ref.at[others], send_sem, recv_sem.at[0], following).wait_send()
+
+    def send_back(comps, pack, out_ref, in_ref, send_sem, recv_sem):
+        start, height = comps[0] * FNODES, len(comps) * FNODES
+        face_traces = jnp.concatenate(
+            [answer[start : start + height, chunk, :] for chunk in range(6)], axis=1
+        )
+        gap = jnp.zeros((LANES - height, FACES), BF16)
+        high, low = split2(face_traces)
+        both = jnp.concatenate([high, gap, low, gap], axis=0)
+        for c in range(N_Y):
+            y = lax.rem(my_y + c, N_Y)
+            found = dot(row_hot[y], both, NT)
+            rows[...] = found[:, 0:LANES] + found[:, LANES : 2 * LANES]
+
+            def send(n, carry):
+                z = lax.rem(my_z + ring_offset(n), N_Z)
+                p = y * N_Z + z
+                base = pl.multiple_of(z * CAP, 8)
+                pack(*thirds(rows[pl.ds(base, CAP), :]), out_ref, p)
+                remote(out_ref.at[p], in_ref.at[me], send_sem, recv_sem.at[c], {"dom": p}).start()
+                return carry
+
+            lax.fori_loop(0, N_Z if c else N_Z - 1, send, 0)
+            if c == 0:
+                base = pl.multiple_of(my_z * CAP, 8)
+                pack(*thirds(rows[pl.ds(base, CAP), :]), in_ref, me)
+
+    def take_traces(comps, unpack, out_ref, in_ref, send_sem, recv_sem):
+        height = len(comps) * FNODES
+        for c in range(N_Y):
+            y = lax.rem(my_y + N_Y - c, N_Y)
+            sources = pl.ds(0, N_Z if c else N_Z - 1)
+            remote(
+                out_ref.at[sources], in_ref.at[sources], send_sem, recv_sem.at[c], following
+            ).wait_recv()
+
+            def take(z, carry):
+                rows[pl.ds(z, CAP, stride=16), :] = jnp.concatenate(unpack(y * N_Z + z), axis=0)
+                return carry
+
+            lax.fori_loop(0, N_Z, take, 0, unroll=2)
+            turned = jnp.transpose(rows[...])[0:height]
+            found = dot(jnp.concatenate(split2(turned), axis=0), slot_hot[y], NN)
+            found = found[0:height] + found[height:]
+            for n, comp in enumerate(comps):
+                for j in range(EFACES):
+                    piece = found[n * FNODES : (n + 1) * FNODES, j * LANES : (j + 1) * LANES]
+                    at = slice(j * FNODES, (j + 1) * FNODES)
+                    traces_ref[comp, at, :] = piece if c == 0 else traces_ref[comp, at, :] + piece
+        remote(out_ref.at[others], in_ref.at[others], send_sem, recv_sem.at[0], following).wait_send()
+
+    early = tuple(range(EARLY))
+    late = tuple(range(EARLY, COMPS))
+    take_rest(first_out, first_in, send_e, recv_e, lambda p: unpack_first(first_in[p]))
+    to_grid(joined_b, LANES, 40)
     first = face_ref[0:1, :]
     idle = jnp.concatenate(
         [first[:, chunk * LANES : (chunk + 1) * LANES] for chunk in range(6)]
         + [jnp.full((2, LANES), ROWS, I32)],
         axis=0,
     )
-    idle = jnp.where(idle < ROWS, 0.0, 1.0)
-    solved = solve_faces(grid, idle)
-    for i in range(FNODES):
-        for comp in range(COMPS):
-            answer[comp * FNODES + i] = solved[i][comp]
-    face_traces = jnp.concatenate([answer[:, chunk, :] for chunk in range(6)], axis=1)
-    gap = jnp.zeros((LANES - COMPS * FNODES, FACES), BF16)
-    high, low = split2(face_traces)
-    both = jnp.concatenate([high, gap, low, gap], axis=0)
-
-    for c in range(N_Y):
-        y = lax.rem(my_y + c, N_Y)
-        found = dot(row_hot[y], both, NT)
-        rows[...] = found[:, 0:LANES] + found[:, LANES : 2 * LANES]
-
-        def send_traces(n, carry):
-            z = lax.rem(my_z + ring_offset(n), N_Z)
-            p = y * N_Z + z
-            pack_traces(rows, z, returning, p)
-            remote(returning.at[p], back.at[me], send_f, recv_f.at[c], {"dom": p}).start()
-            return carry
-
-        lax.fori_loop(0, N_Z if c else N_Z - 1, send_traces, 0)
-        if c == 0:
-            pack_traces(rows, my_z, back, me)
-
-    for c in range(N_Y):
-        y = lax.rem(my_y + N_Y - c, N_Y)
-        sources = pl.ds(0, N_Z if c else N_Z - 1)
-        remote(returning.at[sources], back.at[sources], send_f, recv_f.at[c], following).wait_recv()
-
-        def take_traces(z, carry):
-            unpack_traces(back, y * N_Z + z, rows, z)
-            return carry
-
-        lax.fori_loop(0, N_Z, take_traces, 0, unroll=2)
-        turned = jnp.transpose(rows[...])[0 : COMPS * FNODES]
-        stacked = jnp.concatenate(split2(turned), axis=0)
-        found = dot(stacked, slot_hot[y], NN)
-        found = found[0 : COMPS * FNODES] + found[COMPS * FNODES :]
-        for comp in range(COMPS):
-            for j in range(EFACES):
-                piece = found[comp * FNODES : (comp + 1) * FNODES, j * LANES : (j + 1) * LANES]
-                at = slice(j * FNODES, (j + 1) * FNODES)
-                traces_ref[comp, at, :] = piece if c == 0 else traces_ref[comp, at, :] + piece
-    remote(rest_out.at[others], rest_in.at[others], send_e, recv_e.at[0], following).wait_send()
-    remote(returning.at[others], back.at[others], send_f, recv_f.at[0], following).wait_send()
+    factor_faces(grid, jnp.where(idle < ROWS, 0.0, 1.0), lower, inverse)
+    solve_faces(grid, lower, inverse, early, answer)
+    send_back(early, pack32, early_out, early_in, send_f, recv_f)
+    take_rest(
+        loads_out,
+        loads_in,
+        send_g,
+        recv_g,
+        lambda p: unpack48(loads_in[p, 0:8, :], loads_in[p, 8:9, :]),
+    )
+    to_grid(joined_b, LANES + 40, HALF)
+    solve_faces(grid, lower, inverse, late, answer)
+    send_back(late, pack48, late_out, late_in, send_h, recv_h)
+    take_traces(early, lambda q: unpack32(early_in[q]), early_out, early_in, send_f, recv_f)
+    take_traces(
+        late,
+        lambda q: unpack48(late_in[q, 0:8, :], late_in[q, 8:9, :]),
+        late_out,
+        late_in,
+        send_h,
+        recv_h,
+    )
 
 
 def update_kernel(traces_in, coef_ref, coupling_ref, inner_ref, update_ref, traces_ref):
@@ -678,8 +759,8 @@
     traces, coef = pl.pallas_call(
         step_kernel,
         out_shape=(
-            jax.ShapeDtypeStruct((COMPS, TRACE, LANES), F32),
-            jax.ShapeDtypeStruct((MODES, LANES), F32),
+            pltpu.VMEM((COMPS, TRACE, LANES), F32),
+            pltpu.VMEM((MODES, LANES), F32),
         ),
         in_specs=[anywhere] * 10,
         out_specs=(vmem, vmem),
@@ -704,21 +785,28 @@
             pltpu.VMEM((N_GROUP, 1, LANES), F32),
             pltpu.VMEM((N_Y, PART, SLOTS), BF16),
             pltpu.VMEM((N_Y, PART, FACES), BF16),
-            pltpu.VMEM((LANES, SLOTS), F32),
+            pltpu.VMEM((EFACES, MODES, TRI, LANES), F32),
+            pltpu.VMEM((CAP, N_DOM, LANES), F32),
             pltpu.VMEM((LANES, SLOTS), F32),
             pltpu.VMEM((3 * LANES, SLOTS), BF16),
             pltpu.VMEM((3 * LANES, SLOTS), BF16),
             pltpu.VMEM((PART, LANES), F32),
             pltpu.VMEM((N_DOM, CAP, LANES), F32),
             pltpu.VMEM((N_DOM, CAP, LANES), F32),
-            pltpu.VMEM((N_DOM, REST_TILE, LANES), F32),
-            pltpu.VMEM((N_DOM, REST_TILE, LANES), F32),
+            pltpu.VMEM((N_DOM, FIRST_TILE, LANES), F32),
+            pltpu.VMEM((N_DOM, FIRST_TILE, LANES), F32),
+            pltpu.VMEM((N_DOM, LOAD_TILE, LANES), F32),
+            pltpu.VMEM((N_DOM, LOAD_TILE, LANES), F32),
             pltpu.VMEM((LANES, FACES), F32),
             pltpu.VMEM((HALF, FACES), F32),
             pltpu.VMEM((USED, 8, LANES), F32),
+            pltpu.VMEM((TRI, 8, LANES), F32),
+            pltpu.VMEM((FNODES, 8, LANES), F32),
             pltpu.VMEM((COMPS * FNODES, 8, LANES), F32),
-            pltpu.VMEM((N_DOM, RET_TILE, LANES), F32),
-            pltpu.VMEM((N_DOM, RET_TILE, LANES), F32),
+            pltpu.VMEM((N_DOM, EARLY_TILE, LANES), F32),
+            pltpu.VMEM((N_DOM, EARLY_TILE, LANES), F32),
+            pltpu.VMEM((N_DOM, LATE_TILE, LANES), F32),
+            pltpu.VMEM((N_DOM, LATE_TILE, LANES), F32),
             dma((10,)),
             dma,
             dma,
@@ -726,6 +814,10 @@
             dma,
             dma,
             dma,
+            dma,
+            dma((N_Y,)),
+            dma,
+            dma((N_Y,)),
             dma,
             dma((N_Y,)),
             dma,

time: 131 us -> 130 us (level); the launches traced: 130 us -> 130 us
  Pallas kernels: 127 us -> 129 us
  local copies, waits for them, and re-layouts: 1.7 us -> 0.01 us
    pallas_call x1, Pallas kernels: 125 us -> 127 us  [local(): pl.pallas_call(step_kernel, out_shape=(pltpu.VMEM((COMPS, TRACE, LANES),...]
    unnamed x8 -> x4, local copies, waits for them, and re-layouts: 1.7 us -> 0.01 us
where the time goes in v4:
time: 130 us
  Pallas kernels  129 us (99%)
    pallas_call x1, Pallas kernels, local(): pl.pallas_call(step_kernel, out_shape=(pltpu.VMEM((COMPS, TRACE, LANES),...  127 us

profile of v4, /device:TPU:24, one launch (start us, length us, event | category | flops | bytes accessed | tf_op | source)
XLA Modules:
  0.0 130.0 jit_solution(4537156962562060690)
XLA Ops:
  0.6 0.0 copy-start.1
  0.6 0.0 copy-start
  0.7 126.9 %newton_step.1 = (f32[5,96,128]{2,1,0:T(8,128)S(1)}, f32[64,128]{1,0:T(8,128)S(1)}) custom-call(f32[64,128]{1,0:T(8,128)} %density_hbm.1, f32[1,128]{1,0:T(1,128)} %bitcast.6, s32[1,128]{1,0:T(1,128)} %bitcast.7, f32[1,128]{1,0:T(1,128)} %bitcast.8, f32[1,64]{1,0:T(1,128)} %bitcast.9, s32[12,128]{1,0:T(8,128)} %bitcast.5, s32[2,768]{1,0:T(2,128)} %face_hbm.1, ...), custom_call_target="tpu_custom_call" | custom-call | tf_op jit(solution)/shard_map/newton_step/pallas_call | solution.py:759
  127.5 0.0 copy-done.1
  127.5 0.0 copy-done
  127.6 2.4 %back_substitute.1 = (f32[5,64,128]{2,1,0:T(8,128)}, f32[5,96,128]{2,1,0:T(8,128)}) custom-call(f32[5,96,128]{2,1,0:T(8,128)S(1)} %get-tuple-element.4.traces_in, f32[64,128]{1,0:T(8,128)S(1)} %get-tuple-element.5.coef_ref, bf16[64,96,128]{2,1,0:T(8,128)(2,1)S(1)} %copy-done, f32[5,64,128]{2,1,0:T(8,128)S(1)} %copy-done.1), custom_call_target="tpu_custom_call" | custom-call | tf_op jit(solution)/shard_map/back_substitute/pallas_call | solution.py:844
Async XLA Ops:
  0.6 126.9 %copy-start.1 = (f32[5,64,128]{2,1,0:T(8,128)S(1)}, f32[5,64,128]{2,1,0:T(8,128)}, u32[]{:S(2)}) copy-start(f32[5,64,128]{2,1,0:T(8,128)} %inner_ref.1) | copy-start | bytes 491524
  0.6 126.9 %copy-start = (bf16[64,96,128]{2,1,0:T(8,128)(2,1)S(1)}, bf16[64,96,128]{2,1,0:T(8,128)(2,1)}, u32[]{:S(2)}) copy-start(bf16[64,96,128]{2,1,0:T(8,128)(2,1)} %coupling_ref.1) | copy-start | bytes 4718596

commit v5 on v3

--- a/solution.py
+++ b/solution.py
@@ -143,35 +143,40 @@
     return 128 + (high if base else low)
 
 
-def condense_blocks(coef_ref, coupling_ref, pay_a, pay_b):
+def multiply_blocks(coupling_ref, products):
     sub = iota((8, LANES), 0)
-    for j in range(EFACES):
-
-        def body(k, sums):
-            coef = coef_ref[pl.ds(k, 1), :]
+
+    def body(k, carry):
+        for j in range(EFACES):
             c = coupling_ref[k, j * FNODES : (j + 1) * FNODES, :].astype(F32)
             c0, c1 = c[0:8], c[8:16]
-            u0, u1 = c0 * coef, c1 * coef
-            new = []
-            for d in range(5):
-                new.append(sums[len(new)] + u0 * (pltpu.roll(c0, 8 - d, 0) if d else c0))
-            for d in range(5):
-                new.append(sums[len(new)] + u1 * (pltpu.roll(c1, 8 - d, 0) if d else c1))
+            turned = [c1] + [pltpu.roll(c1, 8 - d, 0) for d in range(1, 8)]
+            for d in range(4):
+                products[j, k, d * 8 : d * 8 + 8, :] = c0 * (pltpu.roll(c0, 8 - d, 0) if d else c0)
+                products[j, k, 32 + d * 8 : 40 + d * 8, :] = c1 * turned[d]
             for d in range(8):
-                new.append(sums[len(new)] + u0 * (pltpu.roll(c1, 8 - d, 0) if d else c1))
-            return tuple(new)
-
-        zero = jnp.zeros((8, LANES), F32)
-        start = [zero] * 18
-        start[0] = start[5] = zero + TAU_STAB
-        sums = lax.fori_loop(0, MODES, body, tuple(start), unroll=8)
+                products[j, k, 64 + d * 8 : 72 + d * 8, :] = c0 * turned[d]
+            products[j, k, 128:136, :] = jnp.where(
+                sub < 4, c0 * pltpu.roll(c0, 4, 0), c1 * turned[4]
+            )
+        return carry
+
+    lax.fori_loop(0, MODES, body, 0)
+
+
+def condense_blocks(coef_ref, products, parts_a, pay_b):
+    for j in range(EFACES):
+
+        def body(k, sums):
+            return sums + coef_ref[pl.ds(k, 1), :] * products[j, k]
+
+        row = iota((TRI, LANES), 0)
+        diagonal = jnp.logical_or(row < 8, jnp.logical_and(row >= 32, row < 40))
+        start = jnp.where(diagonal, TAU_STAB, 0.0)
+        sums = lax.fori_loop(0, MODES, body, start, unroll=8)
         at = pl.ds(j * LANES, LANES)
-        for d in range(4):
-            pay_a[pl.ds(d * 8, 8), at] = sums[d]
-            pay_a[pl.ds(32 + d * 8, 8), at] = sums[5 + d]
-        for d in range(8):
-            pay_a[pl.ds(64 + d * 8, 8), at] = sums[10 + d]
-        pay_b[pl.ds(0, 8), at] = jnp.where(sub < 4, sums[4], sums[9])
+        parts_a[:, at] = jnp.concatenate(split3(sums[0:LANES]), axis=0)
+        pay_b[pl.ds(0, 8), at] = sums[LANES:TRI]
 
 
 def condense_loads(weighted_ref, coupling_ref, face_ref, pay_b):
@@ -348,7 +353,8 @@
     tops,
     slot_hot,
     row_hot,
-    pay_a,
+    products,
+    masks,
     pay_b,
     parts_a,
     parts_b,
@@ -417,9 +423,9 @@
                 (flags_hbm, flags),
                 (send_hbm, lists),
                 (face_hbm, face_ref),
+                (coupling_hbm, coupling),
                 (mass_hbm, mass),
                 (eigs_hbm, eigs_ref),
-                (coupling_hbm, coupling),
                 (inner_hbm, inner),
                 (faceres_hbm, faceres),
             )
@@ -454,10 +460,11 @@
     )
     eps_in[me] = eps_out[me]
     partner_p, partner_i = partner_rows(face_ref)
+    loads[5].wait()
+    multiply_blocks(coupling, products)
     others = pl.ds(0, N_DOM - 1)
-    whole = remote(eps_out.at[others], eps_in.at[others], send_a, recv_a, following)
-    whole.wait_recv()
-    whole.wait_send()
+    first_leg = remote(eps_out.at[others], eps_in.at[others], send_a, recv_a, following)
+    first_leg.wait_recv()
 
     partner_eps = jnp.zeros((16, LANES), F32)
     top = jnp.zeros((1, LANES), F32)
@@ -485,30 +492,30 @@
         row_hot[y] = one_hot(
             jnp.logical_or(received == face_ref[0:1, :], received == face_ref[1:2, :])
         )
-    for copy in loads[5:]:
+    for i in range(CAP):
+        slot = slots[:, i : i + 1]
+        here = jnp.logical_and((slot & (ELEM_DEV - 1)) == lane, slot < SLOTS)
+        masks[i] = jnp.where(here, 1.0, 0.0)
+    for copy in loads[6:]:
         copy.wait()
 
-    whole = remote(eps_in.at[others], visc_in.at[others], send_b, recv_b, following)
-    whole.wait_recv()
-    whole.wait_send()
+    second_leg = remote(eps_in.at[others], visc_in.at[others], send_b, recv_b, following)
+    second_leg.wait_recv()
     seven = pl.ds(0, N_GROUP - 1)
-    whole = remote(
+    top_leg = remote(
         tops.at[seven],
         tops.at[seven],
         send_c,
         recv_c,
         {"group": lax.rem(group + 1, N_GROUP)},
     )
-    whole.wait_recv()
-    whole.wait_send()
+    top_leg.wait_recv()
 
     came = jnp.concatenate([visc_in[q] for q in range(N_DOM)], axis=0)
     came = pltpu.roll(came, lax.rem(4 - lax.rem(me, 4), 4) * 32, 1)
     total = jnp.zeros((N_DOM, LANES), F32)
     for i in range(CAP):
-        slot = slots[:, i : i + 1]
-        here = jnp.logical_and((slot & (ELEM_DEV - 1)) == lane, slot < SLOTS)
-        total = total + jnp.where(here, came[:, i : i + 1], 0.0)
+        total = total + masks[i] * came[:, i : i + 1]
     gathered = jnp.sum(total, axis=0, keepdims=True)
     nu = NU_BASE + (EFACES * eps + gathered) / (2.0 * EFACES)
     top = tops[0]
@@ -520,8 +527,7 @@
     coef = 1.0 / (mass[...] * (1.0 + speed / peak + nu * eigs))
     coef_ref[...] = coef
 
-    condense_blocks(coef_ref, coupling, pay_a, pay_b)
-    parts_a[...] = jnp.concatenate(split3(pay_a[...]), axis=0)
+    condense_blocks(coef_ref, products, parts_a, pay_b)
     for c in range(N_Y):
         y = lax.rem(my_y + c, N_Y)
         rows[...] = pick(slot_hot[y], parts_a[...])
@@ -573,7 +579,6 @@
         found = found[0:LANES] + found[LANES : 2 * LANES] + found[2 * LANES :]
         joined_a[...] = found if c == 0 else joined_a[...] + found
     to_grid(joined_a, 0, LANES)
-    remote(whole_out.at[others], whole_in.at[others], send_d, recv_d.at[0], following).wait_send()
     for c in range(N_Y):
         y = lax.rem(my_y + N_Y - c, N_Y)
         sources = pl.ds(0, N_Z if c else N_Z - 1)
@@ -644,6 +649,9 @@
                 traces_ref[comp, at, :] = piece if c == 0 else traces_ref[comp, at, :] + piece
     remote(rest_out.at[others], rest_in.at[others], send_e, recv_e.at[0], following).wait_send()
     remote(returning.at[others], back.at[others], send_f, recv_f.at[0], following).wait_send()
+    for leg in (first_leg, second_leg, top_leg):
+        leg.wait_send()
+    remote(whole_out.at[others], whole_in.at[others], send_d, recv_d.at[0], following).wait_send()
 
 
 def update_kernel(traces_in, coef_ref, coupling_ref, inner_ref, update_ref, traces_ref):
@@ -678,8 +686,8 @@
     traces, coef = pl.pallas_call(
         step_kernel,
         out_shape=(
-            jax.ShapeDtypeStruct((COMPS, TRACE, LANES), F32),
-            jax.ShapeDtypeStruct((MODES, LANES), F32),
+            pltpu.VMEM((COMPS, TRACE, LANES), F32),
+            pltpu.VMEM((MODES, LANES), F32),
         ),
         in_specs=[anywhere] * 10,
         out_specs=(vmem, vmem),
@@ -704,7 +712,8 @@
             pltpu.VMEM((N_GROUP, 1, LANES), F32),
             pltpu.VMEM((N_Y, PART, SLOTS), BF16),
             pltpu.VMEM((N_Y, PART, FACES), BF16),
-            pltpu.VMEM((LANES, SLOTS), F32),
+            pltpu.VMEM((EFACES, MODES, TRI, LANES), F32),
+            pltpu.VMEM((CAP, N_DOM, LANES), F32),
             pltpu.VMEM((LANES, SLOTS), F32),
             pltpu.VMEM((3 * LANES, SLOTS), BF16),
             pltpu.VMEM((3 * LANES, SLOTS), BF16),

time: 131 us -> 127 us (0.969)
  local copies, waits for them, and re-layouts: 1.7 us -> 0.01 us
    unnamed x8 -> x4, local copies, waits for them, and re-layouts: 1.7 us -> 0.01 us
    pallas_call x1, Pallas kernels: 125 us -> 123 us  [local(): pl.pallas_call(step_kernel, out_shape=(pltpu.VMEM((COMPS, TRACE, LANES),...]
where the time goes in v5:
time: 127 us; the launch traced here: 126 us
  Pallas kernels  126 us (99%)
    pallas_call x1, Pallas kernels, local(): pl.pallas_call(step_kernel, out_shape=(pltpu.VMEM((COMPS, TRACE, LANES),...  123 us

profile of v5, /device:TPU:24, one launch (start us, length us, event | category | flops | bytes accessed | tf_op | source)
XLA Modules:
  0.0 126.2 jit_solution(4094902953872762492)
XLA Ops:
  0.6 0.0 copy-start.1
  0.6 0.0 copy-start
  0.7 123.1 %newton_step.1 = (f32[5,96,128]{2,1,0:T(8,128)S(1)}, f32[64,128]{1,0:T(8,128)S(1)}) custom-call(f32[64,128]{1,0:T(8,128)} %density_hbm.1, f32[1,128]{1,0:T(1,128)} %bitcast.6, s32[1,128]{1,0:T(1,128)} %bitcast.7, f32[1,128]{1,0:T(1,128)} %bitcast.8, f32[1,64]{1,0:T(1,128)} %bitcast.9, s32[12,128]{1,0:T(8,128)} %bitcast.5, s32[2,768]{1,0:T(2,128)} %face_hbm.1, ...), custom_call_target="tpu_custom_call" | custom-call | tf_op jit(solution)/shard_map/newton_step/pallas_call | solution.py:686
  123.8 0.0 copy-done.1
  123.8 0.0 copy-done
  123.8 2.4 %back_substitute.1 = (f32[5,64,128]{2,1,0:T(8,128)}, f32[5,96,128]{2,1,0:T(8,128)}) custom-call(f32[5,96,128]{2,1,0:T(8,128)S(1)} %get-tuple-element.4.traces_in, f32[64,128]{1,0:T(8,128)S(1)} %get-tuple-element.5.coef_ref, bf16[64,96,128]{2,1,0:T(8,128)(2,1)S(1)} %copy-done, f32[5,64,128]{2,1,0:T(8,128)S(1)} %copy-done.1), custom_call_target="tpu_custom_call" | custom-call | tf_op jit(solution)/shard_map/back_substitute/pallas_call | solution.py:761
Async XLA Ops:
  0.6 123.1 %copy-start.1 = (f32[5,64,128]{2,1,0:T(8,128)S(1)}, f32[5,64,128]{2,1,0:T(8,128)}, u32[]{:S(2)}) copy-start(f32[5,64,128]{2,1,0:T(8,128)} %inner_ref.1) | copy-start | bytes 491524
  0.6 123.1 %copy-start = (bf16[64,96,128]{2,1,0:T(8,128)(2,1)S(1)}, bf16[64,96,128]{2,1,0:T(8,128)(2,1)}, u32[]{:S(2)}) copy-start(bf16[64,96,128]{2,1,0:T(8,128)(2,1)} %coupling_ref.1) | copy-start | bytes 4718596

commit v6 on v5

--- a/solution.py
+++ b/solution.py
@@ -21,6 +21,7 @@
 USED = 216
 N_Z = 16
 N_Y = N_DOM // N_Z
+Y_ORDER = (2, 1, 3, 0)
 PART = N_Z * CAP
 LANES = 128
 HALF = 96
@@ -529,7 +530,7 @@
 
     condense_blocks(coef_ref, products, parts_a, pay_b)
     for c in range(N_Y):
-        y = lax.rem(my_y + c, N_Y)
+        y = lax.rem(my_y + Y_ORDER[c], N_Y)
         rows[...] = pick(slot_hot[y], parts_a[...])
 
         def send_whole(n, carry):
@@ -539,14 +540,14 @@
             remote(whole_out.at[q], whole_in.at[me], send_d, recv_d.at[c], {"dom": q}).start()
             return carry
 
-        lax.fori_loop(0, N_Z if c else N_Z - 1, send_whole, 0)
-        if c == 0:
+        lax.fori_loop(0, N_Z if Y_ORDER[c] else N_Z - 1, send_whole, 0)
+        if Y_ORDER[c] == 0:
             whole_in[me] = rows[pl.ds(my_z, CAP, stride=16), :]
     weighted[...] = inner[...] * coef[None]
     condense_loads(weighted, coupling, faceres, pay_b)
     parts_b[...] = jnp.concatenate(split3(pay_b[...]), axis=0)
     for c in range(N_Y):
-        y = lax.rem(my_y + c, N_Y)
+        y = lax.rem(my_y + Y_ORDER[c], N_Y)
         rows[...] = pick(slot_hot[y], parts_b[...])
 
         def send_rest(n, carry):
@@ -556,8 +557,8 @@
             remote(rest_out.at[q], rest_in.at[me], send_e, recv_e.at[c], {"dom": q}).start()
             return carry
 
-        lax.fori_loop(0, N_Z if c else N_Z - 1, send_rest, 0)
-        if c == 0:
+        lax.fori_loop(0, N_Z if Y_ORDER[c] else N_Z - 1, send_rest, 0)
+        if Y_ORDER[c] == 0:
             pack_rest(rows, my_z, rest_in, me)
 
     def to_grid(joined, start, height):
@@ -568,8 +569,8 @@
                 ]
 
     for c in range(N_Y):
-        y = lax.rem(my_y + N_Y - c, N_Y)
-        sources = pl.ds(0, N_Z if c else N_Z - 1)
+        y = lax.rem(my_y + N_Y - Y_ORDER[c], N_Y)
+        sources = pl.ds(0, N_Z if Y_ORDER[c] else N_Z - 1)
         remote(
             whole_out.at[sources], whole_in.at[sources], send_d, recv_d.at[c], following
         ).wait_recv()
@@ -580,8 +581,8 @@
         joined_a[...] = found if c == 0 else joined_a[...] + found
     to_grid(joined_a, 0, LANES)
     for c in range(N_Y):
-        y = lax.rem(my_y + N_Y - c, N_Y)
-        sources = pl.ds(0, N_Z if c else N_Z - 1)
+        y = lax.rem(my_y + N_Y - Y_ORDER[c], N_Y)
+        sources = pl.ds(0, N_Z if Y_ORDER[c] else N_Z - 1)
         remote(
             rest_out.at[sources], rest_in.at[sources], send_e, recv_e.at[c], following
         ).wait_recv()
@@ -613,7 +614,7 @@
     both = jnp.concatenate([high, gap, low, gap], axis=0)
 
     for c in range(N_Y):
-        y = lax.rem(my_y + c, N_Y)
+        y = lax.rem(my_y + Y_ORDER[c], N_Y)
         found = dot(row_hot[y], both, NT)
         rows[...] = found[:, 0:LANES] + found[:, LANES : 2 * LANES]
 
@@ -624,13 +625,13 @@
             remote(returning.at[p], back.at[me], send_f, recv_f.at[c], {"dom": p}).start()
             return carry
 
-        lax.fori_loop(0, N_Z if c else N_Z - 1, send_traces, 0)
-        if c == 0:
+        lax.fori_loop(0, N_Z if Y_ORDER[c] else N_Z - 1, send_traces, 0)
+        if Y_ORDER[c] == 0:
             pack_traces(rows, my_z, back, me)
 
     for c in range(N_Y):
-        y = lax.rem(my_y + N_Y - c, N_Y)
-        sources = pl.ds(0, N_Z if c else N_Z - 1)
+        y = lax.rem(my_y + N_Y - Y_ORDER[c], N_Y)
+        sources = pl.ds(0, N_Z if Y_ORDER[c] else N_Z - 1)
         remote(returning.at[sources], back.at[sources], send_f, recv_f.at[c], following).wait_recv()
 
         def take_traces(z, carry):
@@ -665,7 +666,7 @@
             update_ref[comp, pl.ds(k, 1), :] = coef * (inner_ref[comp, pl.ds(k, 1), :] - pulled)
         return carry
 
-    lax.fori_loop(0, MODES, substitute, 0, unroll=4)
+    lax.fori_loop(0, MODES, substitute, 0, unroll=8)
 
 
 def local(

time: 127 us -> 127 us (level)
  Pallas kernels: 126 us -> 124 us
where the time goes in v6:
time: 127 us; the launch traced here: 125 us
  Pallas kernels  124 us (98%)
    pallas_call x1, Pallas kernels, local(): pl.pallas_call(step_kernel, out_shape=(pltpu.VMEM((COMPS, TRACE, LANES),...  122 us

profile of v6, /device:TPU:24, one launch (start us, length us, event | category | flops | bytes accessed | tf_op | source)
XLA Modules:
  0.0 125.0 jit_solution(4131318534480129200)
XLA Ops:
  0.6 0.0 copy-start.1
  0.6 0.0 copy-start
  0.7 122.0 %newton_step.1 = (f32[5,96,128]{2,1,0:T(8,128)S(1)}, f32[64,128]{1,0:T(8,128)S(1)}) custom-call(f32[64,128]{1,0:T(8,128)} %density_hbm.1, f32[1,128]{1,0:T(1,128)} %bitcast.6, s32[1,128]{1,0:T(1,128)} %bitcast.7, f32[1,128]{1,0:T(1,128)} %bitcast.8, f32[1,64]{1,0:T(1,128)} %bitcast.9, s32[12,128]{1,0:T(8,128)} %bitcast.5, s32[2,768]{1,0:T(2,128)} %face_hbm.1, ...), custom_call_target="tpu_custom_call" | custom-call | tf_op jit(solution)/shard_map/newton_step/pallas_call | solution.py:687
  122.7 0.0 copy-done.1
  122.7 0.0 copy-done
  122.7 2.3 %back_substitute.1 = (f32[5,64,128]{2,1,0:T(8,128)}, f32[5,96,128]{2,1,0:T(8,128)}) custom-call(f32[5,96,128]{2,1,0:T(8,128)S(1)} %get-tuple-element.4.traces_in, f32[64,128]{1,0:T(8,128)S(1)} %get-tuple-element.5.coef_ref, bf16[64,96,128]{2,1,0:T(8,128)(2,1)S(1)} %copy-done, f32[5,64,128]{2,1,0:T(8,128)S(1)} %copy-done.1), custom_call_target="tpu_custom_call" | custom-call | tf_op jit(solution)/shard_map/back_substitute/pallas_call | solution.py:762
Async XLA Ops:
  0.6 122.0 %copy-start.1 = (f32[5,64,128]{2,1,0:T(8,128)S(1)}, f32[5,64,128]{2,1,0:T(8,128)}, u32[]{:S(2)}) copy-start(f32[5,64,128]{2,1,0:T(8,128)} %inner_ref.1) | copy-start | bytes 491524
  0.6 122.0 %copy-start = (bf16[64,96,128]{2,1,0:T(8,128)(2,1)S(1)}, bf16[64,96,128]{2,1,0:T(8,128)(2,1)}, u32[]{:S(2)}) copy-start(bf16[64,96,128]{2,1,0:T(8,128)(2,1)} %coupling_ref.1) | copy-start | bytes 4718596
